TPU v7x, 512 devices: a whole 4x8x8 slice. The times are simulated.
512 devices in a mesh: ind: 32 (over x, y), gene: 16 (over z, core).
Axes of the slice: x: 4, y: 8, z: 8, core: 2. Of those that a mesh axis runs over, the one named last changes fastest.
Arguments:
- genotypes: int32 [32768, 8192], P('ind', 'gene'), may hold values from 0 to 2
- covariates: float32 [20, 32768], P(None, 'ind'), may hold values from -6 to 6
- proteins: bfloat16 [32768, 1664], P('ind', 'gene'), may hold values from -6 to 6
- gene_device: int32 [32], replicated, may hold values from 0 to 15, as said below
- tile_len: int32 [32], replicated, may hold values from 16 to 128, as said below
Outputs:
- burden_z: float32 [32, 1664], P('gene', 'ind')
- skat_q: float32 [32, 1664], P('gene', 'ind')
- cov_blocks: float32 [32, 128, 128], P('gene', 'ind')
Inputs may be any that keep to these rules, and one draw needn't show every extreme that they name: `gene_device`: each index of gene is named by at most 4 genes, and some are named by exactly 4. `tile_len`: some gene has all 128 variants live.
All inputs are finite; a program needn't handle non-finite values.
Results may differ from a plain program's by a relative error of at most 0.0031.
Values may be sent and summed in bfloat16 or wider, within the bound.
A program may use at most 64 MiB of HBM per device.

v0:
```python
import math

import jax
import jax.numpy as jnp
from jax import lax
from jax.sharding import Mesh
from jax.sharding import PartitionSpec as P

COV = 20
TV = 128
IND = ("ind_0", "ind_1")


highest_value = lax.Precision.HIGHEST


def copy_for_each(value, axis):
    peers = lax.axis_size(axis)
    return lax.all_to_all(
        jnp.broadcast_to(value[None], (peers, *value.shape)), axis, 0, 0, tiled=True
    )


def over_copies(value, axis):
    return copy_for_each(value, axis).sum(axis=0)


def together(arrays, axis):
    ends = [0]
    for a in arrays:
        ends.append(ends[-1] + a.size)
    subtotal = over_copies(jnp.concatenate([a.ravel() for a in arrays]), axis)
    return tuple((subtotal[b:e].reshape(a.shape) for a, b, e in zip(arrays, ends, ends[1:])))


def sum_by_axis(value, axes, dim):
    if not axes:
        return value
    nearer = lax.psum_scatter(value, axes[0], scatter_dimension=dim, tiled=True)
    return sum_by_axis(nearer, axes[1:], dim)


def in_one_piece(arrays, axis, dim, along):
    widths = [math.prod(a.shape[along:]) for a in arrays]
    both = jnp.concatenate(
        [a.reshape(*a.shape[:along], w) for a, w in zip(arrays, widths)], axis=along
    )
    filled = lax.all_gather(both, axis, axis=dim, tiled=True)
    blocks = jnp.split(filled, [sum(widths[:k]) for k in range(1, len(widths))], axis=along)
    return tuple(
        (b.reshape(*filled.shape[:along], *a.shape[along:]) for a, b in zip(arrays, blocks))
    )


def solve_moments(gram_matrix, rhs):
    factor = jnp.linalg.cholesky(gram_matrix)
    return jax.scipy.linalg.cho_solve((factor, True), rhs)


def per_device(genotypes, covariates, proteins, gene_device, tile_len):
    local_rows = genotypes.shape[0]
    slot_count = genotypes.shape[1] // TV
    gene_total = gene_device.shape[0]
    gene_index = lax.axis_index("gene")
    gene_axis = lax.axis_size("gene")
    total_rows = local_rows * lax.axis_size(IND)
    design_width = COV + 1
    gene_order = jnp.arange(gene_total, dtype=jnp.int32)
    before = (gene_device[None, :] == gene_device[:, None]) & (
        gene_order[None, :] < gene_order[:, None]
    )
    slot_rank = jnp.sum(before.astype(jnp.int32), axis=1)
    placement = (
        (gene_device[:, None] == gene_index)
        & (slot_rank[:, None] == jnp.arange(slot_count, dtype=jnp.int32)[None, :])
    ).astype(jnp.float32)
    slot_len = jnp.dot(tile_len.astype(jnp.float32), placement, precision=highest_value)
    live_mask = (jnp.arange(TV, dtype=jnp.float32)[None, :] < slot_len[:, None]).astype(jnp.int32)
    allele_tally = (
        (genotypes.reshape(local_rows, slot_count, TV) * live_mask[None])
        .reshape(local_rows, slot_count * TV)
        .astype(jnp.float32)
    )
    design = jnp.concatenate([jnp.ones((1, local_rows), jnp.float32), covariates], axis=0)
    gram_local = jnp.dot(design, design.T, precision=highest_value)
    geno_local = jnp.dot(design, allele_tally, precision=highest_value)
    traits_local = jnp.dot(design, proteins.astype(jnp.float32), precision=highest_value)
    gram_matrix, cross_traits, cross_geno = together((gram_local, traits_local, geno_local), IND)
    trait_coef = solve_moments(gram_matrix, cross_traits)
    own_resid = (
        proteins.astype(jnp.float32) - jnp.dot(design.T, trait_coef, precision=highest_value)
    ).astype(jnp.bfloat16)
    trait_resid = lax.all_gather(own_resid, "gene", axis=1, tiled=True)
    geno_coef = solve_moments(gram_matrix, cross_geno)
    geno_resid = (allele_tally - jnp.dot(design.T, geno_coef, precision=highest_value)).astype(
        jnp.bfloat16
    )
    allele_freq = cross_geno[0] / (2.0 * total_rows)
    weight = 25.0 * (1.0 - allele_freq) ** 24 * live_mask.reshape(-1).astype(jnp.float32)
    weight_grid = weight.reshape(slot_count, TV)
    scores_local = lax.dot_general(
        geno_resid, trait_resid, (((0,), (0,)), ((), ())), preferred_element_type=jnp.float32
    )
    geno_tiles = geno_resid.reshape(local_rows, slot_count, TV)
    cov_local = jnp.einsum(
        "isu,isv->suv", geno_tiles, geno_tiles, preferred_element_type=jnp.float32
    )
    square_local = jnp.sum(jnp.square(trait_resid.astype(jnp.float32)), axis=0)
    tile_values = geno_tiles.astype(jnp.float32)
    burden_rows = jnp.einsum("isv,sv->is", tile_values, weight_grid, precision=highest_value)
    burden_local = jnp.sum(jnp.square(burden_rows), axis=0)
    dosage_local = jnp.sum(jnp.square(tile_values), axis=0).reshape(slot_count * TV)
    scores, covariance, square_part = (
        sum_by_axis(scores_local, IND, 1),
        sum_by_axis(cov_local, IND, 1),
        sum_by_axis(square_local[None, :], IND, 1),
    )
    square_sum = square_part[0]
    burden_sums, dosage_sums = together((burden_local, dosage_local), IND)
    variance = square_sum / (total_rows - design_width) + 1e-05
    score_grid = scores.reshape(slot_count, TV, -1)
    burden_den = 1.0 + burden_sums
    skat_den = 1.0 + jnp.sum(
        weight_grid * weight_grid * dosage_sums.reshape(slot_count, TV), axis=1
    )
    burden_score = jnp.einsum("svp,sv->sp", score_grid, weight_grid, precision=highest_value)
    skat_score = jnp.einsum(
        "svp,sv->sp", score_grid * score_grid, weight_grid * weight_grid, precision=highest_value
    )
    burden_slot = burden_score / jnp.sqrt(burden_den[:, None] * variance[None, :])
    skat_slot = skat_score / (skat_den[:, None] * variance[None, :])
    slot_stats = jnp.stack([burden_slot, skat_slot], axis=1)
    cov_slot = covariance / total_rows
    genes_owned = gene_total // gene_axis
    whole_test_outputs, all_cov = in_one_piece((slot_stats, cov_slot), "gene", 0, 1)
    global_slot = gene_device * slot_count + slot_rank
    target_slot = lax.dynamic_slice_in_dim(global_slot, gene_index * genes_owned, genes_owned)
    column_picker = (
        target_slot[:, None] == jnp.arange(gene_axis * slot_count, dtype=jnp.int32)[None, :]
    ).astype(jnp.float32)
    owned_statistics = jnp.einsum(
        "xw,wie->xie", column_picker, whole_test_outputs, precision=highest_value
    )
    owned_cov = jnp.einsum("gs,srv->grv", column_picker, all_cov, precision=highest_value)
    return (owned_statistics[:, 0, :], owned_statistics[:, 1, :], owned_cov)


def solution(mesh):
    split = Mesh(mesh.devices.reshape(4, 8, mesh.shape["gene"]), ("ind_0", "ind_1", "gene"))
    placed = (P(IND, "gene"), P(None, IND), P(IND, "gene"), P(), P())
    return jax.shard_map(
        per_device,
        mesh=split,
        in_specs=placed,
        out_specs=(P("gene", IND), P("gene", IND), P("gene", IND, None)),
        check_vma=False,
    )
```

profile of v0, /device:TPU:1, one launch (start us, length us, event | category | flops | bytes accessed | tf_op | source)
XLA Modules:
  0.0 324.1 jit_solution(14201200776618932549)
XLA Ops:
  8.0 0.9 convert_reduce_fusion
  9.0 0.7 broadcast_compare_fusion
  9.6 0.8 convolution_bitcast_fusion
  10.6 1.2 fusion.18
  11.8 1.3 fusion.16
  13.0 0.1 reshape.134
  13.1 0.1 reshape.133
  13.2 2.0 copy.35
  15.2 1.9 fusion.1
  17.1 0.1 concatenate.13
  17.2 0.9 broadcast_in_dim.6
  18.1 49.8 %all_to_all.12 = f32[32,1,13377]{2,1,0:T(1,128)} all-to-all(f32[32,1,13377]{2,1,0:T(1,128)S(1)} %broadcast_in_dim.6), channel_id=1, replica_groups=mesh['ind_0'=4,'ind_1'=8,'gene'=16] {'ind_0','ind_1'}, dimensions={0} | all-to-all | bytes 3424512 | tf_op jit(solution)/shard_map/all_to_all | solution.py:19
  67.9 2.4 reduce_sum.64
  70.4 0.1 slice.73
  70.5 0.1 reshape.136
  70.6 0.1 copy.37
  70.7 1.9 cholesky.18
  72.6 0.6 compare_reduce_fusion
  73.3 0.6 fusion.26
  73.9 1.6 custom-call.15
  75.5 0.1 reshape.138
  75.7 0.2 fusion.33
  75.9 0.2 fusion.31
  76.1 2.2 multiply_reduce_fusion.1
  78.2 1.1 fusion.65
  79.5 0.2 fusion.29
  79.7 0.1 fusion.27
  79.8 1.2 fusion.4
  81.1 26.3 %reduce-scatter.12.cloned.1.call-done = f32[4,32,128]{2,1,0:T(8,128)} async-done(((f32[4,128,128]{2,1,0:T(8,128)}), f32[4,32,128]{2,1,0:T(8,128)}) %reduce-scatter.12.cloned.1.call-update) | async-done | bytes 65552 | tf_op jit(solution)/shard_map/reduce_scatter | solution.py:39
  107.5 22.8 %all-gather.3.cloned.1.call-done = bf16[1024,1664]{0,1:T(8,128)(2,1)} async-done(((bf16[1024,104]{0,1:T(8,128)(2,1)}), bf16[1024,1664]{0,1:T(8,128)(2,1)}) %all-gather.3.cloned.1.call-update) | async-done | bytes 3407888 | tf_op jit(solution)/shard_map/all_gather | solution.py:93
  130.3 2.7 multiply_reduce_fusion
  133.0 1.2 reshape_bitcast_fusion
  134.3 5.7 %fusion.63 = f32[512,1664]{0,1:T(8,128)} fusion(bf16[1024,512]{0,1:T(8,128)(2,1)S(1)} %get-tuple-element.28, bf16[1024,1664]{0,1:T(8,128)(2,1)} %all-gather.3.cloned.1.call-done), kind=kOutput, calls=%fused_computation.99 | convolution fusion | flops 1744830464 | bytes 7864320 | tf_op jit(solution)/shard_map/dot_general | solution.py:101
  140.0 0.6 copy-done.2
  140.6 0.6 fusion.62
  143.1 0.1 fusion.60
  143.2 0.5 fusion.64
  143.7 0.1 fusion.22
  143.9 0.1 pad_maximum_fusion
  143.9 0.7 broadcast_in_dim.7
  144.6 9.5 %all-to-all-start.1 = ((f32[32,1,516]{2,1,0:T(1,128)}), f32[32,1,516]{2,1,0:T(1,128)S(1)}, u32[]{:S(2)}, u32[]{:S(2)}) async-start(f32[32,1,516]{2,1,0:T(1,128)} %broadcast_in_dim.7), calls=%async_computation.2 | async-start | bytes 163840 | tf_op jit(solution)/shard_map/all_to_all | solution.py:19
  154.2 0.1 dynamic_slice.3
  154.3 8.8 %all-to-all-done.1 = f32[32,1,516]{2,1,0:T(1,128)S(1)} async-done(((f32[32,1,516]{2,1,0:T(1,128)}), f32[32,1,516]{2,1,0:T(1,128)S(1)}, u32[]{:S(2)}, u32[]{:S(2)}) %all-to-all-start.1) | async-done | bytes 66080 | tf_op jit(solution)/shard_map/all_to_all | solution.py:19
  163.2 0.2 fusion.46
  163.4 20.8 %all-reduce.7.cloned.1.call-done = f32[4,32,128]{2,1,0:T(8,128)} async-done(((f32[4,32,128]{2,1,0:T(8,128)}), f32[4,32,128]{2,1,0:T(8,128)}) %all-reduce.7.cloned.1.call-update) | async-done | bytes 65552
  184.2 0.7 fusion.36
  184.9 32.7 %reduce-scatter.14.cloned.1.call-done = f32[416,1]{1,0:T(8,128)} async-done(((f32[1664,1]{1,0:T(8,128)}), f32[416,1]{1,0:T(8,128)}) %reduce-scatter.14.cloned.1.call-update) | async-done | bytes 1680
  217.7 1.0 copy.53
  218.7 13.4 %all-reduce.2 = f32[1,416]{1,0:T(1,128)S(1)} all-reduce(f32[1,416]{1,0:T(1,128)S(1)} %copy.53), channel_id=5, replica_groups=mesh['ind_0'=4,'ind_1'=8,'gene'=16] {'ind_1'}, use_global_device_ids=true, to_apply=%region_11.13.clone | all-reduce | flops 416 | bytes 3328
  232.1 35.0 %reduce-scatter.10.cloned.1.call-done = f32[512,416]{0,1:T(8,128)} async-done(((f32[512,1664]{0,1:T(8,128)}), f32[512,416]{0,1:T(8,128)}) %reduce-scatter.10.cloned.1.call-update) | async-done | bytes 851984 | tf_op jit(solution)/shard_map/reduce_scatter | solution.py:39
  267.1 20.4 %fusion = f32[512,56]{0,1:T(8,128)S(1)} fusion(f32[512,416]{0,1:T(8,128)} %reduce-scatter.10.cloned.1.call-done), kind=kCustom, calls=%all-reduce-scatter | all-reduce-scatter fusion | flops 229377 | bytes 968704
  287.5 1.6 collective-permute-start
  289.1 0.1 fusion.54
  289.2 1.2 collective-permute-done
  290.4 0.1 concatenate.16
  290.7 0.3 fusion.11
  291.0 0.3 fusion.9
  291.4 0.1 reshape.142
  291.5 23.6 %all-gather = f32[16,4,616]{2,1,0:T(4,128)S(1)} all-gather(f32[1,4,616]{2,1,0:T(4,128)S(1)} %maximum_bitcast_fusion), channel_id=1, replica_groups=mesh['ind_0'=4,'ind_1'=8,'gene'=16] {'gene'}, dimensions={0}, use_global_device_ids=true | all-gather | bytes 167552 | tf_op jit(solution)/shard_map/all_gather | solution.py:48
  315.2 0.2 fusion.6
  315.5 0.6 copy.43
  316.1 0.1 reshape.144
  316.2 0.2 fusion.20
  316.4 0.6 slice_bitcast_fusion.1
  (38 shorter events, 1.0 us)
Async XLA Ops:
  8.0 99.4 %reduce-scatter.12.cloned.1.call-start = ((), (), s32[]{:S(2)}) async-start(), calls=%async_computation.7 | async-start | bytes 327680 | tf_op jit(solution)/shard_map/reduce_scatter | solution.py:39
  13.2 2.0 copy-start
  78.2 1.6 copy-start.1
  79.4 50.9 %all-gather.3.cloned.1.call-start = ((), (), s32[]{:S(2)}) async-start(), calls=%async_computation.5 | async-start | bytes 3620864 | tf_op jit(solution)/shard_map/all_gather | solution.py:93
  81.1 103.1 %all-reduce.7.cloned.1.call-start = ((), (), s32[]{:S(2)}) async-start(), calls=%async_computation.9 | async-start | bytes 131072
  107.5 110.2 %reduce-scatter.14.cloned.1.call-start = ((), (), s32[]{:S(2)}) async-start(), calls=%async_computation.8 | async-start | bytes 1064960
  134.2 132.9 %reduce-scatter.10.cloned.1.call-start = ((), (), s32[]{:S(2)}) async-start(), calls=%async_computation.6 | async-start | bytes 4259840 | tf_op jit(solution)/shard_map/reduce_scatter | solution.py:39
  139.9 0.7 copy-start.2
  139.9 14.2 %copy-start.3 = (s32[32]{0:T(128)S(1)}, s32[32]{0:T(128)}, u32[]{:S(2)}) copy-start(s32[32]{0:T(128)} %param.9) | copy-start | bytes 388
  144.6 18.5 %all-to-all-start.1 = ((f32[32,1,516]{2,1,0:T(1,128)}), f32[32,1,516]{2,1,0:T(1,128)S(1)}, u32[]{:S(2)}, u32[]{:S(2)}) async-start(f32[32,1,516]{2,1,0:T(1,128)} %broadcast_in_dim.7), calls=%async_computation.2 | async-start | bytes 163840 | tf_op jit(solution)/shard_map/all_to_all | solution.py:19
  287.5 2.9 collective-permute-start
Sparse Core Ops, SparseCore 0:
  79.5 27.8 reduce-scatter.11
  109.7 74.3 all-reduce.6
  187.0 30.5 reduce-scatter.13
  220.4 46.7 reduce-scatter.9
Sparse Core Ops, SparseCore 1:
  82.0 48.2 all-gather.2
where the time goes:
time: 325 us; the launch traced here: 324 us
  waiting for transfers between devices  148 us (46%)
  blocking collectives  107 us (33%)
  matrix products  17.6 us (5%)
  between operations  17.4 us (5%)
  other arithmetic  13.2 us (4%)
  starting transfers between devices  11.4 us (4%)
  local copies, waits for them, and re-layouts  9.58 us (3%)
    reduce_scatter x2, waiting for transfers between devices, sum_by_axis(): nearer = lax.psum_scatter(value, axes[0], scatter_dimension=dim, tiled=True)  61.3 us
    unnamed x8, waiting for transfers between devices  54.9 us
    all_to_all x1, blocking collectives, copy_for_each(): lax.all_to_all(jnp.broadcast_to(value[None], (peers, *value.shape)), axis...  49.8 us
    unnamed x2, blocking collectives  33.8 us
    all_gather x1, blocking collectives, in_one_piece(): filled = lax.all_gather(both, axis, axis=dim, tiled=True)  23.6 us
    all_gather x1, waiting for transfers between devices, per_device(): trait_resid = lax.all_gather(own_resid, 'gene', axis=1, tiled=True)  22.8 us
    all_to_all x1, starting transfers between devices, copy_for_each(): lax.all_to_all(jnp.broadcast_to(value[None], (peers, *value.shape)), axis...  9.53 us
    all_to_all x1, waiting for transfers between devices, copy_for_each(): lax.all_to_all(jnp.broadcast_to(value[None], (peers, *value.shape)), axis...  8.84 us
  transfers between devices with their start and end apart: 7, of which 7 were waited for; matrix products, arithmetic and copies ran while one was open for 5% of the time, Pallas kernels for 0%

commit v1 on v0

v1 whole, which is shorter than its diff:
```python
import functools

import jax
import jax.numpy as jnp
from jax import lax
from jax.experimental import pallas as pl
from jax.experimental.pallas import tpu as pltpu
from jax.sharding import PartitionSpec as P

COV = 20
WIDTH = COV + 1
TV = 128
SLOTS = 4
NX = 4
ROWS = 56
BLOCK = 64
COV_ROWS = 4
TILES = 18

BF = jnp.bfloat16
F32 = jnp.float32
HIGHEST = lax.Precision.HIGHEST
MESH = pl.DeviceIdType.MESH


def dot(a, b, form="nn", precision=None):
    dims = {"nn": ((1,), (0,)), "nt": ((1,), (1,)), "tn": ((0,), (0,))}[form]
    return lax.dot_general(a, b, (dims, ((), ())), precision=precision, preferred_element_type=F32)


def split3(v):
    hi = v.astype(BF).astype(F32)
    rest = v - hi
    mid = rest.astype(BF).astype(F32)
    return hi, mid, (rest - mid).astype(BF).astype(F32)


def iota(shape, dim):
    return lax.broadcasted_iota(jnp.int32, shape, dim)


def kernel(
    ni, ng, half, units,
    geno_ref, cov_ref, prot_ref, mask_ref, pick_ref,
    bz_ref, sq_ref, cv_ref,
    g_s, gb_s, gr_s, d_s, dst_s, dct_s, tall, stat_s, part_s, psum_s, total_s, call_s,
    ext_s, p_s, sbuf, relay_in, relay_out, from_one, from_two, yout, yin, fin_s, fall,
    load_sem, t_send, t_recv, pair_send, pair_recv, own_send, own_recv,
    rs_send, rs_recv, ag_send, ag_recv, c_send, c_recv, x_send, x_recv, y_send, y_recv,
    f_send, f_recv,
):
    ind, gene = lax.axis_index("ind"), lax.axis_index("gene")
    ny, nz = ni // NX, ng // 2
    x, y = lax.div(ind, ny), lax.rem(ind, ny)
    z, core = lax.div(gene, 2), lax.rem(gene, 2)
    rows, pt = prot_ref.shape
    half_rows = rows // 2
    per_chunk = ni // ng
    n_total = rows * ni
    lanes = SLOTS * TV
    per_unit = TILES // units

    def remote(src, dst, send, recv, i, g):
        return pltpu.make_async_remote_copy(
            src_ref=src, dst_ref=dst, send_sem=send, recv_sem=recv,
            device_id=(i, g), device_id_type=MESH,
        )

    load = pltpu.make_async_copy(geno_ref, g_s, load_sem)
    load.start()
    barrier = pltpu.get_barrier_semaphore()

    @pl.loop(1, ni)
    def _(d):
        pl.semaphore_signal(
            barrier, inc=1, device_id=(lax.rem(ind + d, ni), gene), device_id_type=MESH
        )

    @pl.loop(1, ng)
    def _(d):
        pl.semaphore_signal(
            barrier, inc=1, device_id=(ind, lax.rem(gene + d, ng)), device_id_type=MESH
        )

    eye = (iota((pt, pt), 0) == iota((pt, pt), 1)).astype(F32).astype(BF)
    tt = dot(eye, prot_ref[...], "nt").astype(BF)
    tall[gene, 0] = tt[:, :half_rows]
    tall[gene, 1] = tt[:, half_rows:]
    pl.semaphore_wait(barrier, ni + ng - 2)

    def ring(way, step, q):
        sign = 1 if way == 0 else -1
        chunk = lax.rem(z - sign * (step - 1) + 2 * nz, nz) * 2 + core
        target = lax.rem(z + sign + nz, nz) * 2 + core
        return remote(
            tall.at[chunk, q], tall.at[chunk, q],
            t_send.at[way, step - 1, q], t_recv.at[way, step - 1, q], ind, target,
        )

    def across(way, step, q):
        sign = 1 if way == 0 else -1
        chunk = lax.rem(z - sign * step + 2 * nz, nz) * 2 + core
        return remote(
            tall.at[chunk, q], tall.at[chunk, q],
            pair_send.at[way, step - 1, q], pair_recv.at[way, step - 1, q],
            ind, z * 2 + 1 - core,
        )

    def moves(step):
        if step < nz // 2:
            return [(way, q) for q in range(2) for way in range(2)]
        return [(0, 0), (1, 1)]

    own_copy = remote(tall.at[gene], tall.at[gene], own_send, own_recv, ind, z * 2 + 1 - core)
    for way, q in moves(1):
        ring(way, 1, q).start()
    own_copy.start()

    def forward(step):
        for way, q in moves(step):
            ring(way, step, q).wait_recv()
            if step < nz // 2 and (way, q) in moves(step + 1):
                ring(way, step + 1, q).start()
            across(way, step, q).start()

    d_s[...] = jnp.zeros_like(d_s)
    d_s[0:1, :] = jnp.ones((1, rows), F32)
    d_s[1 : 1 + COV, :] = cov_ref[...]
    design = d_s[...]
    d1, d2, d3 = split3(design)
    dst_s[...] = jnp.concatenate([d1, d2, d3], axis=0).astype(BF)
    mask = mask_ref[...]
    load.wait()
    step_rows = min(128, rows)

    @pl.loop(0, rows // step_rows)
    def _(b):
        at = pl.ds(pl.multiple_of(b * step_rows, step_rows), step_rows)
        gb_s[at, :] = (g_s[at, :].astype(F32) * mask).astype(BF)

    wide = dot(dst_s[...], gb_s[...])
    dg = wide[0:32] + wide[32:64] + wide[64:96]
    tall_own = jnp.concatenate([tall[gene, 0], tall[gene, 1]], axis=1)
    narrow = dot(dst_s[...], tall_own, "nt")
    dt = narrow[0:32] + narrow[32:64] + narrow[64:96]
    square = jnp.square(tall_own.astype(F32))
    sq_hi = square.astype(BF)
    sq_lo = (square - sq_hi.astype(F32)).astype(BF)
    ones = jnp.ones((16, rows), BF)
    t2 = dot(ones, sq_hi, "nt") + dot(ones, sq_lo, "nt")
    dt = dt[0:24] + jnp.where(iota((24, pt), 0) == WIDTH, t2[0:1], 0.0)
    gram = dot(design, design, "nt", HIGHEST)
    stat_s[...] = jnp.zeros_like(stat_s)
    for r in range(3):
        sub = slice(8 * r, 8 * r + 8)
        for c in range(SLOTS):
            k = r * SLOTS + c
            at = slice(8 * (k % per_unit), 8 * (k % per_unit) + 8)
            stat_s[k // per_unit, at, :] = dg[sub, TV * c : TV * c + TV]
        k = 12 + r
        at = slice(8 * (k % per_unit), 8 * (k % per_unit) + 8)
        stat_s[k // per_unit, at, 0:pt] = dt[sub]
        k = 15 + r
        at = slice(8 * (k % per_unit), 8 * (k % per_unit) + 8)
        stat_s[k // per_unit, at, 0:32] = gram[sub]

    def to_owner(t):
        return remote(
            stat_s.at[t], part_s.at[lax.rem(ind - t + ni, ni)], rs_send, rs_recv, t, gene
        )

    @pl.loop(0, units)
    def _(t):
        @pl.when(t != ind)
        def _():
            to_owner(t).start()

    dcat = jnp.concatenate([d1, d2, d3, d1, d2, d1, jnp.zeros((64, rows), F32)], axis=0)
    dct_s[...] = jnp.transpose(dcat).astype(BF)
    forward(1)

    @pl.when(ind < units)
    def _():
        part_s[0] = stat_s[ind]
        got = part_s.at[pl.ds(1, ni - 1)]
        remote(got, got, rs_send, rs_recv, ind, gene).wait_recv()
        subtotal = jnp.sum(part_s[...], axis=0)
        psum_s[...] = subtotal
        total_s[ind] = subtotal

        @pl.loop(1, ni)
        def _(d):
            remote(
                psum_s, total_s.at[ind], ag_send, ag_recv, lax.rem(ind + d, ni), gene
            ).start()

    if nz // 2 >= 2:
        forward(2)

    @pl.when(ind < units)
    def _():
        got = total_s.at[pl.ds(0, units - 1)]
        remote(got, got, ag_send, ag_recv, ind, gene).wait_recv()

    @pl.when(ind >= units)
    def _():
        remote(total_s, total_s, ag_send, ag_recv, ind, gene).wait_recv()

    def tile(k):
        return total_s[k // per_unit, 8 * (k % per_unit) : 8 * (k % per_unit) + 8, :]

    cross_geno = jnp.concatenate(
        [jnp.concatenate([tile(r * SLOTS + c) for c in range(SLOTS)], axis=1) for r in range(3)],
        axis=0,
    )
    traits = jnp.concatenate([tile(12 + r) for r in range(3)], axis=0)
    gram_sum = jnp.concatenate([tile(15 + r) for r in range(3)], axis=0)
    t2_sum = traits[WIDTH : WIDTH + 1]
    cross_traits = jnp.where(iota((24, TV), 0) < WIDTH, traits, 0.0)
    work = jnp.concatenate([gram_sum, cross_geno, cross_traits], axis=1)
    row_id = iota(work.shape, 0)
    for k in range(WIDTH):
        pivot = work[k : k + 1] / work[k : k + 1, k : k + 1]
        work = jnp.where(row_id == k, pivot, work - work[:, k : k + 1] * pivot)
    geno_coef = work[:, TV : TV + lanes]
    trait_coef = work[:, TV + lanes :]
    variance = (t2_sum - jnp.sum(cross_traits * trait_coef, axis=0, keepdims=True)) / (
        n_total - WIDTH
    ) + 1e-05
    v1, v2, v3 = split3(variance)
    sub8 = iota((8, TV), 0)
    tail = jnp.where(sub8 == 0, v1, jnp.where(sub8 == 1, v2, jnp.where(sub8 == 2, v3, 0.0)))
    call_s[gene] = jnp.concatenate([trait_coef, tail], axis=0).astype(BF)

    @pl.loop(1, ng)
    def _(d):
        remote(
            call_s.at[gene], call_s.at[gene], c_send, c_recv, ind, lax.rem(gene + d, ng)
        ).start()

    if nz // 2 >= 3:
        forward(3)
    base = 1.0 - cross_geno[0:1] / (2.0 * n_total)
    b2 = base * base
    b4 = b2 * b2
    b8 = b4 * b4
    weight = 25.0 * (b8 * b8 * b8) * mask

    c1, c2, c3 = split3(jnp.concatenate([geno_coef, jnp.zeros((8, lanes), F32)], axis=0))
    rcat = jnp.concatenate([c1, c1, c1, c2, c2, c3, jnp.zeros((64, lanes), F32)], axis=0).astype(BF)

    @pl.loop(0, rows // step_rows)
    def _(b):
        at = pl.ds(pl.multiple_of(b * step_rows, step_rows), step_rows)
        gr_s[at, :] = (gb_s[at, :].astype(F32) - dot(dct_s[at, :], rcat)).astype(BF)

    wide = dot(dst_s[...], gr_s[...])
    h1, h2, h3 = split3(wide[0:32] + wide[32:64] + wide[64:96])
    hcat = jnp.concatenate([h1, h2, h3], axis=0).astype(BF)

    sel_r, sel_c = iota((ni * 8, TV), 0), iota((ni * 8, TV), 1)
    sub = lax.rem(sel_r, 8)
    sel = jnp.where((sub < COV_ROWS) & (sel_c == lax.div(sel_r, 8) * COV_ROWS + sub), 1.0, 0.0)
    sel = sel.astype(BF)
    diag = iota((TV, TV), 0) == iota((TV, TV), 1)
    for s in range(SLOTS):
        cols = slice(s * TV, s * TV + TV)
        tile_r = gr_s[:, cols]
        cov_s = dot(tile_r, tile_r, "tn")
        w = weight[:, cols]
        wc = dot(jnp.broadcast_to(w, (8, TV)), cov_s, "nn", HIGHEST)
        burden = jnp.sum(wc[0:1] * w, axis=1, keepdims=True)
        dosage = jnp.sum(jnp.where(diag, cov_s, 0.0), axis=0, keepdims=True)
        skat = jnp.sum(dosage * w * w, axis=1, keepdims=True)
        b_hi, b_lo, _ = split3(burden)
        k_hi, k_lo, _ = split3(skat)
        ext = dot(sel, cov_s.astype(BF))
        ext = jnp.where(sub == 4, b_hi, jnp.where(sub == 5, b_lo, ext))
        ext = jnp.where(sub == 6, k_hi, jnp.where(sub == 7, k_lo, ext))
        ext_s[s] = ext.reshape(ni, 8, TV)

    for step in range(4, nz // 2 + 1):
        forward(step)
    got = call_s.at[pl.ds(0, ng - 1)]
    remote(got, got, c_send, c_recv, ind, gene).wait_recv()
    own_copy.wait_recv()
    for step in range(1, nz // 2 + 1):
        for way, q in moves(step):
            across(way, step, q).wait_recv()

    p_s[...] = jnp.zeros_like(p_s)

    @pl.loop(0, ng)
    def _(j):
        cj = call_s[j]
        fix = dot(jnp.concatenate([cj, cj, cj], axis=0), hcat, "tn")
        p_s[0:pt, :] = (
            dot(tall[j, 0], gr_s[0:half_rows, :])
            + dot(tall[j, 1], gr_s[half_rows:, :])
            - fix[0:pt]
        )
        for kk in range(per_chunk):
            i = j * per_chunk + kk
            for s in range(SLOTS):
                part = p_s[kk * half : kk * half + ROWS, s * TV : s * TV + TV]
                sbuf[s, i] = jnp.concatenate([part, ext_s[s, i]], axis=0).astype(BF)

    def unit(s, to):
        return sbuf.at[s, pl.ds(lax.rem(to + NX, NX) * ny, ny)]

    def x_copy(s, which):
        sign = 1 if s % 2 == 0 else -1
        ahead = lax.rem(x + sign + NX, NX) * ny + y
        behind = lax.rem(x - sign + NX, NX) * ny + y
        src, dst, to = (
            (lambda: unit(s, x + 2), relay_in, ahead),
            (lambda: unit(s, x - sign), from_one, behind),
            (lambda: relay_out.at[s], from_two, ahead),
        )[which]
        return remote(src(), dst.at[s], x_send.at[s, which], x_recv.at[s, which], to, gene)

    def y_copy(s, d):
        to = lax.rem(y + d, ny)
        return remote(
            yout.at[s, to], yin.at[s, ny - d], y_send.at[s], y_recv.at[s], x * ny + to, gene
        )

    def relay(s):
        sign = 1 if s % 2 == 0 else -1
        x_copy(s, 0).wait_recv()
        to = lax.rem(x + sign + NX, NX) * ny

        @pl.loop(0, ny)
        def _(b):
            relay_out[s, b] = (relay_in[s, b].astype(F32) + sbuf[s, to + b].astype(F32)).astype(BF)

        x_copy(s, 2).start()

    def over_x(s, b):
        return (
            sbuf[s, x * ny + b].astype(F32)
            + from_one[s, b].astype(F32)
            + from_two[s, b].astype(F32)
        )

    def gather_x(s):
        x_copy(s, 1).wait_recv()
        x_copy(s, 2).wait_recv()

        @pl.loop(0, ny)
        def _(b):
            yout[s, b] = over_x(s, b).astype(BF)

        @pl.loop(1, ny)
        def _(d):
            y_copy(s, d).start()

    for s in range(SLOTS):
        x_copy(s, 0).start()
        x_copy(s, 1).start()
    relay(0)
    relay(1)
    gather_x(0)
    relay(2)
    gather_x(1)
    relay(3)
    gather_x(2)
    gather_x(3)

    vrow = call_s[lax.div(ind, per_chunk)].astype(F32)[24:32]
    vrow = jnp.broadcast_to(vrow[0:1] + vrow[1:2] + vrow[2:3], (8, TV))
    var = vrow
    for kk in range(1, per_chunk):
        var = jnp.where(lax.rem(ind, per_chunk) == kk, pltpu.roll(vrow, TV - kk * half, 1), var)
    var = var[0:1, 0:ROWS]
    fin_s[...] = jnp.zeros_like(fin_s)
    for s in range(SLOTS):
        got = yin.at[s, pl.ds(1, ny - 1)]
        remote(got, got, y_send.at[s], y_recv.at[s], ind, gene).wait_recv()
        whole = over_x(s, y)
        for d in range(1, ny):
            whole = whole + yin[s, d].astype(F32)
        score = whole[0:ROWS]
        w = jnp.broadcast_to(weight[:, s * TV : s * TV + TV], (8, TV))
        burden = dot(w, score, "nt", HIGHEST)[0:1]
        skat = dot(w * w, score * score, "nt", HIGHEST)[0:1]
        b_den = 1.0 + whole[60:61, 0:ROWS] + whole[61:62, 0:ROWS]
        k_den = 1.0 + whole[62:63, 0:ROWS] + whole[63:64, 0:ROWS]
        fin_s[s : s + 1, 0:ROWS] = burden / jnp.sqrt(b_den * var)
        fin_s[4 + s : 5 + s, 0:ROWS] = skat / (k_den * var)
        up = 4 * (s // 2)
        left = TV + TV * (s % 2)
        fin_s[up : up + 4, left : left + TV] = whole[56:60] * (1.0 / n_total)

    @pl.loop(1, ng)
    def _(d):
        remote(fin_s, fall.at[ng - d], f_send, f_recv, ind, lax.rem(gene + d, ng)).start()

    fall[0] = fin_s[...]
    got = fall.at[pl.ds(1, ng - 1)]
    remote(got, got, f_send, f_recv, ind, gene).wait_recv()
    flat = fall[...].reshape(ng * 8, 3 * TV)
    stats = dot(pick_ref[0:8], flat[:, 0:TV], "nn", HIGHEST)
    bz_ref[...] = stats[0:2, 0:half]
    sq_ref[...] = stats[2:4, 0:half]
    cov_out = dot(pick_ref[8:16], flat[:, TV : 2 * TV], "nn", HIGHEST) + dot(
        pick_ref[16:24], flat[:, 2 * TV :], "nn", HIGHEST
    )
    cv_ref[0] = cov_out[0:4]
    cv_ref[1] = cov_out[4:8]

    for step in range(1, nz // 2 + 1):
        for way, q in moves(step):
            ring(way, step, q).wait_send()
            across(way, step, q).wait_send()
    own_copy.wait_send()

    @pl.when(ind < units)
    def _():
        got = stat_s.at[pl.ds(0, units - 1)]
        remote(got, got, rs_send, rs_recv, ind, gene).wait_send()
        got = part_s.at[pl.ds(1, ni - 1)]
        remote(got, got, ag_send, ag_recv, ind, gene).wait_send()

    @pl.when(ind >= units)
    def _():
        remote(stat_s, stat_s, rs_send, rs_recv, ind, gene).wait_send()

    got = call_s.at[pl.ds(0, ng - 1)]
    remote(got, got, c_send, c_recv, ind, gene).wait_send()
    for s in range(SLOTS):
        for which in range(3):
            x_copy(s, which).wait_send()
        got = yout.at[s, pl.ds(0, ny - 1)]
        remote(got, got, y_send.at[s], y_recv.at[s], ind, gene).wait_send()
    got = fall.at[pl.ds(1, ng - 1)]
    remote(got, got, f_send, f_recv, ind, gene).wait_send()


def selections(gene_device, tile_len, gene_axis, owned):
    me = lax.axis_index("gene")
    total = gene_device.shape[0]
    order = jnp.arange(total, dtype=jnp.int32)
    before = (gene_device[None, :] == gene_device[:, None]) & (order[None, :] < order[:, None])
    rank = jnp.sum(before.astype(jnp.int32), axis=1)
    slot = jnp.arange(SLOTS * TV, dtype=jnp.int32) // TV
    variant = jnp.arange(SLOTS * TV, dtype=jnp.int32) % TV
    live = (
        (gene_device[:, None] == me)
        & (rank[:, None] == slot[None, :])
        & (variant[None, :] < tile_len[:, None])
    )
    mask = jnp.any(live, axis=0).astype(F32)[None, :]
    mine = order[None, :] == (me * owned + jnp.arange(owned, dtype=jnp.int32))[:, None]
    where = jnp.sum(jnp.where(mine, lax.rem(gene_device - me + gene_axis, gene_axis), 0), axis=1)
    slot_of = jnp.sum(jnp.where(mine, rank, 0), axis=1)
    r = jnp.arange(24, dtype=jnp.int32)[:, None]
    gene_row = jnp.where(r < 8, r % 2, (r - 8) % 8 // 4)
    here = jnp.where(gene_row == 0, where[0], where[1])
    s = jnp.where(gene_row == 0, slot_of[0], slot_of[1])
    stat_col = here * 8 + jnp.where(r < 2, s, 4 + s)
    cov_col = here * 8 + s // 2 * 4 + (r - 8) % 4
    cov_on = s % 2 == (r - 8) // 8
    col = jnp.where(r < 8, stat_col, cov_col)
    on = jnp.where(r < 8, r < 4, cov_on)
    wide = jnp.arange(gene_axis * 8, dtype=jnp.int32)[None, :]
    pick = ((wide == col) & on).astype(F32)
    return mask, pick


def per_device(genotypes, covariates, proteins, gene_device, tile_len):
    ni, ng = lax.axis_size("ind"), lax.axis_size("gene")
    rows, pt = proteins.shape
    lanes = SLOTS * TV
    half = pt * ng // ni
    owned = gene_device.shape[0] // ng
    units = TILES if ni >= TILES else 6
    tall_unit = TILES // units * 8
    ny, nz = ni // NX, ng // 2
    mask, pick = selections(gene_device, tile_len, ng, owned)
    vmem = pl.BlockSpec(memory_space=pltpu.VMEM)
    dma = pltpu.SemaphoreType.DMA
    unit = (SLOTS, ny, BLOCK, TV)
    scratch = [
        pltpu.VMEM((rows, lanes), jnp.int32),
        pltpu.VMEM((rows, lanes), BF),
        pltpu.VMEM((rows, lanes), BF),
        pltpu.VMEM((32, rows), F32),
        pltpu.VMEM((96, rows), BF),
        pltpu.VMEM((rows, 256), BF),
        pltpu.VMEM((ng, 2, pt, rows // 2), BF),
        pltpu.VMEM((units, tall_unit, TV), F32),
        pltpu.VMEM((ni, tall_unit, TV), F32),
        pltpu.VMEM((tall_unit, TV), F32),
        pltpu.VMEM((units, tall_unit, TV), F32),
        pltpu.VMEM((ng, 32, TV), BF),
        pltpu.VMEM((SLOTS, ni, 8, TV), F32),
        pltpu.VMEM((112, lanes), F32),
        pltpu.VMEM((SLOTS, ni, BLOCK, TV), BF),
        pltpu.VMEM(unit, BF),
        pltpu.VMEM(unit, BF),
        pltpu.VMEM(unit, BF),
        pltpu.VMEM(unit, BF),
        pltpu.VMEM(unit, BF),
        pltpu.VMEM(unit, BF),
        pltpu.VMEM((8, 3 * TV), F32),
        pltpu.VMEM((ng, 8, 3 * TV), F32),
        dma,
        dma((2, nz // 2, 2)), dma((2, nz // 2, 2)),
        dma((2, nz // 2, 2)), dma((2, nz // 2, 2)),
        dma, dma, dma, dma, dma, dma, dma, dma,
        dma((SLOTS, 3)), dma((SLOTS, 3)),
        dma((SLOTS,)), dma((SLOTS,)),
        dma, dma,
    ]
    return pl.pallas_call(
        functools.partial(kernel, ni, ng, half, units),
        out_shape=(
            jax.ShapeDtypeStruct((owned, half), F32),
            jax.ShapeDtypeStruct((owned, half), F32),
            jax.ShapeDtypeStruct((owned, COV_ROWS, TV), F32),
        ),
        in_specs=[pl.BlockSpec(memory_space=pl.ANY), vmem, vmem, vmem, vmem],
        out_specs=(vmem, vmem, vmem),
        scratch_shapes=scratch,
        compiler_params=pltpu.CompilerParams(
            collective_id=0, has_side_effects=True, vmem_limit_bytes=48 * 1024 * 1024
        ),
    )(genotypes, covariates, proteins, mask, pick)


def solution(mesh):
    return jax.shard_map(
        per_device,
        mesh=mesh,
        in_specs=(P("ind", "gene"), P(None, "ind"), P("ind", "gene"), P(), P()),
        out_specs=(P("gene", "ind"), P("gene", "ind"), P("gene", "ind", None)),
        check_vma=False,
    )
```

time: 325 us -> 98.5 us (0.30)
  waiting for transfers between devices: 148 us -> 0 us
  blocking collectives: 107 us -> 0 us
  Pallas kernels: 0 us -> 84.3 us
  matrix products: 17.6 us -> 0 us
  between operations: 17.4 us -> 0.68 us
  starting transfers between devices: 11.4 us -> 0 us
  other arithmetic: 13.2 us -> 7.24 us
  local copies, waits for them, and re-layouts: 9.58 us -> 5.91 us
    pallas_call x0 -> x1, Pallas kernels: none -> 84.3 us  [per_device(): pl.pallas_call(functools.partial(kernel, ni, ng, half, units), out_shape=...]
    reduce_scatter x2 -> x0, waiting for transfers between devices: 61.3 us -> none  [sum_by_axis(): nearer = lax.psum_scatter(value, axes[0], scatter_dimension=dim, tiled=True)]
    unnamed x8 -> x0, waiting for transfers between devices: 54.9 us -> none
    all_to_all x1 -> x0, blocking collectives: 49.8 us -> none  [copy_for_each(): lax.all_to_all(jnp.broadcast_to(value[None], (peers, *value.shape)), axis...]
    unnamed x2 -> x0, blocking collectives: 33.8 us -> none
    all_gather x1 -> x0, blocking collectives: 23.6 us -> none  [in_one_piece(): filled = lax.all_gather(both, axis, axis=dim, tiled=True)]
    all_gather x1 -> x0, waiting for transfers between devices: 22.8 us -> none  [per_device(): trait_resid = lax.all_gather(own_resid, 'gene', axis=1, tiled=True)]
    dot_general x13 -> x0, matrix products: 16.8 us -> none  [the longest x1 5.66 us: per_device(): lax.dot_general(geno_resid, trait_resid, (((0,), (0,)), ((), ())), prefer...]
  transfers between devices with their start and end apart: 7 -> 0, of which waited for: 7 -> 0; matrix products, arithmetic and copies ran while one was open for 5% -> 0% of each run, Pallas kernels for 0% -> 0%
where the time goes in v1:
time: 98.5 us; the launch traced here: 98.2 us
  Pallas kernels  84.3 us (86%)
  other arithmetic  7.24 us (7%)
  local copies, waits for them, and re-layouts  5.91 us (6%)
    pallas_call x1, Pallas kernels, per_device(): pl.pallas_call(functools.partial(kernel, ni, ng, half, units), out_shape=...  84.3 us
    unnamed x8, local copies, waits for them, and re-layouts  5.3 us
    select_n x1, other arithmetic, selections(): col = jnp.where(r < 8, stat_col, cov_col)  2.65 us

profile of v1, /device:TPU:1, one launch (start us, length us, event | category | flops | bytes accessed | tf_op | source)
XLA Modules:
  0.0 98.2 jit_solution(553537082866946921)
XLA Ops:
  0.6 0.9 convert_reduce_fusion
  1.6 0.7 broadcast_compare_fusion
  2.2 0.7 compare_select_fusion
  2.9 0.2 select_reduce_fusion
  3.1 0.6 fusion.18
  3.7 2.7 %fusion.14 = s32[24]{0:T(128)S(1)} fusion(s32[]{:T(128)} %bitcast.2, s32[]{:T(128)} %bitcast.1, s32[]{:T(128)} %bitcast.4, s32[]{:T(128)} %bitcast.3), kind=kLoop, calls=%fused_computation.50 | loop fusion | flops 1680 | bytes 112 | tf_op jit(solution)/shard_map/jit(_where)/select_n | solution.py:464
  6.3 1.3 %compare_select_fusion.2 = pred[24]{0:T(512)(128)(4,1)S(1)} fusion(s32[]{:T(128)} %bitcast.4, s32[]{:T(128)} %bitcast.3), kind=kLoop, calls=%fused_computation.20 | loop fusion | flops 1416 | bytes 32 | tf_op jit(solution)/shard_map/jit(_where)/select_n | solution.py:465
  7.7 0.8 and_reduce_fusion
  8.4 0.1 fusion.2.pick_ref
  8.5 1.1 %copy.9.prot_ref = bf16[1024,104]{1,0:T(8,128)(2,1)S(1)} copy(bf16[1024,104]{0,1:T(8,128)(2,1)} %param.7) | data formatting | bytes 425984 | tf_op args[2]
  9.6 0.0 copy-start
  9.6 1.6 %copy-done = s32[1024,512]{1,0:T(8,128)S(1)} copy-done((s32[1024,512]{1,0:T(8,128)S(1)}, s32[1024,512]{1,0:T(8,128)}, u32[]{:S(2)}) %copy-start) | copy-done | bytes 2097176
  11.2 0.0 copy-start.1
  11.2 0.9 copy-done.1
  12.1 84.3 %shard_map.76 = (f32[2,52]{1,0:T(2,128)S(1)}, f32[2,52]{1,0:T(2,128)S(1)}, f32[2,4,128]{2,1,0:T(4,128)S(1)}) custom-call(s32[1024,512]{1,0:T(8,128)S(1)} %copy-done, f32[20,1024]{1,0:T(8,128)S(1)} %copy-done.1, bf16[1024,104]{1,0:T(8,128)(2,1)S(1)} %copy.9.prot_ref, f32[1,512]{1,0:T(1,128)S(1)} %bitcast.5, f32[24,128]{1,0:T(8,128)S(1)} %fusion.2.pick_ref), custom_call_target="tpu_custom_call" | custom-call | tf_op jit(solution)/shard_map/pallas_call | solution.py:516
  96.5 0.6 copy.13
  97.0 0.6 copy.14
  97.6 0.6 copy.15
  (3 shorter events, 0.0 us)
Async XLA Ops:
  9.6 1.6 %copy-start = (s32[1024,512]{1,0:T(8,128)S(1)}, s32[1024,512]{1,0:T(8,128)}, u32[]{:S(2)}) copy-start(s32[1024,512]{1,0:T(8,128)} %geno_ref.1) | copy-start | bytes 6291460
  11.2 0.9 copy-start.1

commit v2 on v1

--- a/solution.py
+++ b/solution.py
@@ -41,7 +41,7 @@
 
 def kernel(
     ni, ng, half, units,
-    geno_ref, cov_ref, prot_ref, mask_ref, pick_ref,
+    geno_ref, cov_ref, prot_ref, home_ref, len_ref,
     bz_ref, sq_ref, cv_ref,
     g_s, gb_s, gr_s, d_s, dst_s, dct_s, tall, stat_s, part_s, psum_s, total_s, call_s,
     ext_s, p_s, sbuf, relay_in, relay_out, from_one, from_two, yout, yin, fin_s, fall,
@@ -53,7 +53,7 @@
     ny, nz = ni // NX, ng // 2
     x, y = lax.div(ind, ny), lax.rem(ind, ny)
     z, core = lax.div(gene, 2), lax.rem(gene, 2)
-    rows, pt = prot_ref.shape
+    pt, rows = prot_ref.shape
     half_rows = rows // 2
     per_chunk = ni // ng
     n_total = rows * ni
@@ -82,10 +82,9 @@
             barrier, inc=1, device_id=(ind, lax.rem(gene + d, ng)), device_id_type=MESH
         )
 
-    eye = (iota((pt, pt), 0) == iota((pt, pt), 1)).astype(F32).astype(BF)
-    tt = dot(eye, prot_ref[...], "nt").astype(BF)
-    tall[gene, 0] = tt[:, :half_rows]
-    tall[gene, 1] = tt[:, half_rows:]
+    tall[gene, 0] = prot_ref[:, :half_rows]
+    tall[gene, 1] = prot_ref[:, half_rows:]
+    mask, pick = selections(home_ref[...], len_ref[...], gene, ng)
     pl.semaphore_wait(barrier, ni + ng - 2)
 
     def ring(way, step, q):
@@ -129,7 +128,6 @@
     design = d_s[...]
     d1, d2, d3 = split3(design)
     dst_s[...] = jnp.concatenate([d1, d2, d3], axis=0).astype(BF)
-    mask = mask_ref[...]
     load.wait()
     step_rows = min(128, rows)
 
@@ -140,7 +138,7 @@
 
     wide = dot(dst_s[...], gb_s[...])
     dg = wide[0:32] + wide[32:64] + wide[64:96]
-    tall_own = jnp.concatenate([tall[gene, 0], tall[gene, 1]], axis=1)
+    tall_own = prot_ref[...]
     narrow = dot(dst_s[...], tall_own, "nt")
     dt = narrow[0:32] + narrow[32:64] + narrow[64:96]
     square = jnp.square(tall_own.astype(F32))
@@ -400,11 +398,11 @@
     got = fall.at[pl.ds(1, ng - 1)]
     remote(got, got, f_send, f_recv, ind, gene).wait_recv()
     flat = fall[...].reshape(ng * 8, 3 * TV)
-    stats = dot(pick_ref[0:8], flat[:, 0:TV], "nn", HIGHEST)
+    stats = dot(pick[0:8], flat[:, 0:TV], "nn", HIGHEST)
     bz_ref[...] = stats[0:2, 0:half]
     sq_ref[...] = stats[2:4, 0:half]
-    cov_out = dot(pick_ref[8:16], flat[:, TV : 2 * TV], "nn", HIGHEST) + dot(
-        pick_ref[16:24], flat[:, 2 * TV :], "nn", HIGHEST
+    cov_out = dot(pick[8:16], flat[:, TV : 2 * TV], "nn", HIGHEST) + dot(
+        pick[16:24], flat[:, 2 * TV :], "nn", HIGHEST
     )
     cv_ref[0] = cov_out[0:4]
     cv_ref[1] = cov_out[4:8]
@@ -437,35 +435,47 @@
     remote(got, got, f_send, f_recv, ind, gene).wait_send()
 
 
-def selections(gene_device, tile_len, gene_axis, owned):
-    me = lax.axis_index("gene")
-    total = gene_device.shape[0]
-    order = jnp.arange(total, dtype=jnp.int32)
-    before = (gene_device[None, :] == gene_device[:, None]) & (order[None, :] < order[:, None])
-    rank = jnp.sum(before.astype(jnp.int32), axis=1)
-    slot = jnp.arange(SLOTS * TV, dtype=jnp.int32) // TV
-    variant = jnp.arange(SLOTS * TV, dtype=jnp.int32) % TV
-    live = (
-        (gene_device[:, None] == me)
-        & (rank[:, None] == slot[None, :])
-        & (variant[None, :] < tile_len[:, None])
+def selections(home, length, me, ng):
+    total = home.shape[1]
+    owned = total // ng
+    g_row, g_col = iota((total, total), 0), iota((total, total), 1)
+    same = g_row == g_col
+
+    def column(row):
+        return jnp.sum(jnp.where(same, row, 0), axis=1, keepdims=True)
+
+    home_col, len_col = column(home), column(length)
+    before = jnp.where((home == home_col) & (g_col < g_row), 1, 0)
+    rank = jnp.sum(before, axis=1, keepdims=True)
+    gene_id = iota((total, 1), 0)
+
+    def chosen(where, value):
+        return jnp.sum(jnp.where(where, value, 0), axis=0, keepdims=True)
+
+    variant = iota((1, TV), 1)
+    live = [
+        jnp.where(variant < chosen((home_col == me) & (rank == s), len_col), 1.0, 0.0)
+        for s in range(SLOTS)
+    ]
+    mask = jnp.concatenate(live, axis=1)
+    far = home_col - me
+    far = jnp.where(far < 0, far + ng, far)
+    here = [chosen(gene_id == me * owned + o, far) for o in range(owned)]
+    slot = [chosen(gene_id == me * owned + o, rank) for o in range(owned)]
+    r, c = iota((24, ng * 8), 0), iota((24, ng * 8), 1)
+    first = jnp.where(r < 8, r % 2, (r - 8) % 8 // 4) == 0
+    at = jnp.where(first, here[0], here[1])
+    s = jnp.where(first, slot[0], slot[1])
+    upper = jnp.where(s < 2, 0, 1)
+    stat_col = at * 8 + jnp.where(r < 2, s, 4 + s)
+    cov_col = at * 8 + upper * 4 + (r - 8) % 4
+    cov_on = (s - upper * 2) == (r - 8) // 8
+    hit = jnp.where(
+        r < 8,
+        jnp.where((c == stat_col) & (r < 4), 1.0, 0.0),
+        jnp.where((c == cov_col) & cov_on, 1.0, 0.0),
     )
-    mask = jnp.any(live, axis=0).astype(F32)[None, :]
-    mine = order[None, :] == (me * owned + jnp.arange(owned, dtype=jnp.int32))[:, None]
-    where = jnp.sum(jnp.where(mine, lax.rem(gene_device - me + gene_axis, gene_axis), 0), axis=1)
-    slot_of = jnp.sum(jnp.where(mine, rank, 0), axis=1)
-    r = jnp.arange(24, dtype=jnp.int32)[:, None]
-    gene_row = jnp.where(r < 8, r % 2, (r - 8) % 8 // 4)
-    here = jnp.where(gene_row == 0, where[0], where[1])
-    s = jnp.where(gene_row == 0, slot_of[0], slot_of[1])
-    stat_col = here * 8 + jnp.where(r < 2, s, 4 + s)
-    cov_col = here * 8 + s // 2 * 4 + (r - 8) % 4
-    cov_on = s % 2 == (r - 8) // 8
-    col = jnp.where(r < 8, stat_col, cov_col)
-    on = jnp.where(r < 8, r < 4, cov_on)
-    wide = jnp.arange(gene_axis * 8, dtype=jnp.int32)[None, :]
-    pick = ((wide == col) & on).astype(F32)
-    return mask, pick
+    return mask, hit
 
 
 def per_device(genotypes, covariates, proteins, gene_device, tile_len):
@@ -477,7 +487,6 @@
     units = TILES if ni >= TILES else 6
     tall_unit = TILES // units * 8
     ny, nz = ni // NX, ng // 2
-    mask, pick = selections(gene_device, tile_len, ng, owned)
     vmem = pl.BlockSpec(memory_space=pltpu.VMEM)
     dma = pltpu.SemaphoreType.DMA
     unit = (SLOTS, ny, BLOCK, TV)
@@ -524,9 +533,9 @@
         out_specs=(vmem, vmem, vmem),
         scratch_shapes=scratch,
         compiler_params=pltpu.CompilerParams(
-            collective_id=0, has_side_effects=True, vmem_limit_bytes=48 * 1024 * 1024
+            collective_id=0, has_side_effects=True, vmem_limit_bytes=66_000_000
         ),
-    )(genotypes, covariates, proteins, mask, pick)
+    )(genotypes, covariates, proteins.T, gene_device[None, :], tile_len[None, :])
 
 
 def solution(mesh):

time: 98.5 us -> 90.2 us (0.916)
  other arithmetic: 7.24 us -> 0 us
  local copies, waits for them, and re-layouts: 5.91 us -> 3.71 us
  Pallas kernels: 84.3 us -> 85.6 us
    select_n x3 -> x0, other arithmetic: 3.98 us -> none  [the longest x1 2.65 us: selections(): col = jnp.where(r < 8, stat_col, cov_col)]
    unnamed x8 -> x3, local copies, waits for them, and re-layouts: 5.3 us -> 3.71 us
    pallas_call x1, Pallas kernels: 84.3 us -> 85.6 us  [per_device(): pl.pallas_call(functools.partial(kernel, ni, ng, half, units), out_shape=...]
    reduce_sum x2 -> x0, other arithmetic: 1.09 us -> none  [the longest x1 0.91 us: selections(): rank = jnp.sum(before.astype(jnp.int32), axis=1)]
where the time goes in v2:
time: 90.2 us; the launch traced here: 90 us
  Pallas kernels  85.6 us (95%)
  local copies, waits for them, and re-layouts  3.71 us (4%)
    pallas_call x1, Pallas kernels, per_device(): pl.pallas_call(functools.partial(kernel, ni, ng, half, units), out_shape=...  85.6 us
    unnamed x3, local copies, waits for them, and re-layouts  3.71 us

profile of v2, /device:TPU:1, one launch (start us, length us, event | category | flops | bytes accessed | tf_op | source)
XLA Modules:
  0.0 90.0 jit_solution(17465726982847711666)
XLA Ops:
  0.6 85.6 %shard_map.76 = (f32[2,52]{1,0:T(2,128)}, f32[2,52]{1,0:T(2,128)}, f32[2,4,128]{2,1,0:T(4,128)}) custom-call(s32[1024,512]{1,0:T(8,128)} %geno_ref.1, f32[20,1024]{1,0:T(8,128)} %cov_ref.1, bf16[104,1024]{1,0:T(8,128)(2,1)} %bitcast.3, s32[1,32]{1,0:T(1,128)} %bitcast.4, s32[1,32]{1,0:T(1,128)} %bitcast.5), custom_call_target="tpu_custom_call" | custom-call | tf_op jit(solution)/shard_map/pallas_call | solution.py:525
  86.2 1.2 %copy.11 = f32[2,52]{1,0:T(2,128)} copy(f32[2,52]{1,0:T(2,128)} %get-tuple-element.6) | data formatting | bytes 832
  87.5 1.2 %copy.12 = f32[2,52]{1,0:T(2,128)} copy(f32[2,52]{1,0:T(2,128)} %get-tuple-element.7) | data formatting | bytes 832
  88.7 1.3 %copy.13 = f32[2,4,128]{2,1,0:T(4,128)} copy(f32[2,4,128]{2,1,0:T(4,128)} %get-tuple-element.8) | data formatting | bytes 8192

commit v3 on v2

--- a/solution.py
+++ b/solution.py
@@ -14,6 +14,7 @@
 NX = 4
 ROWS = 56
 BLOCK = 64
+PAIR = 2
 COV_ROWS = 4
 TILES = 18
 
@@ -44,10 +45,10 @@
     geno_ref, cov_ref, prot_ref, home_ref, len_ref,
     bz_ref, sq_ref, cv_ref,
     g_s, gb_s, gr_s, d_s, dst_s, dct_s, tall, stat_s, part_s, psum_s, total_s, call_s,
-    ext_s, p_s, sbuf, relay_in, relay_out, from_one, from_two, yout, yin, fin_s, fall,
+    ext_s, kx_all, p_s, sbuf, relay_in, relay_out, from_one, from_two, yout, yin, fin_s, fall,
     load_sem, t_send, t_recv, pair_send, pair_recv, own_send, own_recv,
     rs_send, rs_recv, ag_send, ag_recv, c_send, c_recv, x_send, x_recv, y_send, y_recv,
-    f_send, f_recv,
+    k_send, k_recv, f_send, f_recv,
 ):
     ind, gene = lax.axis_index("ind"), lax.axis_index("gene")
     ny, nz = ni // NX, ng // 2
@@ -56,6 +57,8 @@
     pt, rows = prot_ref.shape
     half_rows = rows // 2
     per_chunk = ni // ng
+    padded = per_chunk * ROWS
+    unit_rows = ny * ROWS
     n_total = rows * ni
     lanes = SLOTS * TV
     per_unit = TILES // units
@@ -82,26 +85,33 @@
             barrier, inc=1, device_id=(ind, lax.rem(gene + d, ng)), device_id_type=MESH
         )
 
-    tall[gene, 0] = prot_ref[:, :half_rows]
-    tall[gene, 1] = prot_ref[:, half_rows:]
+    spread_r, spread_c = iota((padded, pt), 0), iota((padded, pt), 1)
+    spread = spread_r - spread_r // ROWS * (ROWS - half) == spread_c
+    spread = jnp.where(spread & (spread_r % ROWS < half), 1.0, 0.0).astype(BF)
+    tall_own = dot(spread, prot_ref[...]).astype(BF)
+    own_rows = pl.ds(pl.multiple_of(gene * padded, padded), padded)
+    tall[0, own_rows, :] = tall_own[:, :half_rows]
+    tall[1, own_rows, :] = tall_own[:, half_rows:]
     mask, pick = selections(home_ref[...], len_ref[...], gene, ng)
     pl.semaphore_wait(barrier, ni + ng - 2)
 
+    def chunk_of(way, step):
+        sign = 1 if way == 0 else -1
+        chunk = lax.rem(z - sign * step + 2 * nz, nz) * 2 + core
+        return pl.ds(pl.multiple_of(chunk * padded, padded), padded)
+
     def ring(way, step, q):
         sign = 1 if way == 0 else -1
-        chunk = lax.rem(z - sign * (step - 1) + 2 * nz, nz) * 2 + core
+        block = tall.at[q, chunk_of(way, step - 1)]
         target = lax.rem(z + sign + nz, nz) * 2 + core
         return remote(
-            tall.at[chunk, q], tall.at[chunk, q],
-            t_send.at[way, step - 1, q], t_recv.at[way, step - 1, q], ind, target,
+            block, block, t_send.at[way, step - 1, q], t_recv.at[way, step - 1, q], ind, target
         )
 
     def across(way, step, q):
-        sign = 1 if way == 0 else -1
-        chunk = lax.rem(z - sign * step + 2 * nz, nz) * 2 + core
+        block = tall.at[q, chunk_of(way, step)]
         return remote(
-            tall.at[chunk, q], tall.at[chunk, q],
-            pair_send.at[way, step - 1, q], pair_recv.at[way, step - 1, q],
+            block, block, pair_send.at[way, step - 1, q], pair_recv.at[way, step - 1, q],
             ind, z * 2 + 1 - core,
         )
 
@@ -110,17 +120,24 @@
             return [(way, q) for q in range(2) for way in range(2)]
         return [(0, 0), (1, 1)]
 
-    own_copy = remote(tall.at[gene], tall.at[gene], own_send, own_recv, ind, z * 2 + 1 - core)
+    def own_copy(q):
+        block = tall.at[q, own_rows]
+        return remote(block, block, own_send.at[q], own_recv.at[q], ind, z * 2 + 1 - core)
+
     for way, q in moves(1):
         ring(way, 1, q).start()
-    own_copy.start()
-
-    def forward(step):
+    for q in range(2):
+        own_copy(q).start()
+
+    def forward(step, half_of):
+        if step > nz // 2:
+            return
         for way, q in moves(step):
-            ring(way, step, q).wait_recv()
-            if step < nz // 2 and (way, q) in moves(step + 1):
-                ring(way, step + 1, q).start()
-            across(way, step, q).start()
+            if q == half_of:
+                ring(way, step, q).wait_recv()
+                if step < nz // 2 and (way, q) in moves(step + 1):
+                    ring(way, step + 1, q).start()
+                across(way, step, q).start()
 
     d_s[...] = jnp.zeros_like(d_s)
     d_s[0:1, :] = jnp.ones((1, rows), F32)
@@ -138,7 +155,6 @@
 
     wide = dot(dst_s[...], gb_s[...])
     dg = wide[0:32] + wide[32:64] + wide[64:96]
-    tall_own = prot_ref[...]
     narrow = dot(dst_s[...], tall_own, "nt")
     dt = narrow[0:32] + narrow[32:64] + narrow[64:96]
     square = jnp.square(tall_own.astype(F32))
@@ -146,7 +162,7 @@
     sq_lo = (square - sq_hi.astype(F32)).astype(BF)
     ones = jnp.ones((16, rows), BF)
     t2 = dot(ones, sq_hi, "nt") + dot(ones, sq_lo, "nt")
-    dt = dt[0:24] + jnp.where(iota((24, pt), 0) == WIDTH, t2[0:1], 0.0)
+    dt = dt[0:24] + jnp.where(iota((24, padded), 0) == WIDTH, t2[0:1], 0.0)
     gram = dot(design, design, "nt", HIGHEST)
     stat_s[...] = jnp.zeros_like(stat_s)
     for r in range(3):
@@ -157,7 +173,7 @@
             stat_s[k // per_unit, at, :] = dg[sub, TV * c : TV * c + TV]
         k = 12 + r
         at = slice(8 * (k % per_unit), 8 * (k % per_unit) + 8)
-        stat_s[k // per_unit, at, 0:pt] = dt[sub]
+        stat_s[k // per_unit, at, 0:padded] = dt[sub]
         k = 15 + r
         at = slice(8 * (k % per_unit), 8 * (k % per_unit) + 8)
         stat_s[k // per_unit, at, 0:32] = gram[sub]
@@ -173,9 +189,11 @@
         def _():
             to_owner(t).start()
 
+    forward(1, 0)
     dcat = jnp.concatenate([d1, d2, d3, d1, d2, d1, jnp.zeros((64, rows), F32)], axis=0)
     dct_s[...] = jnp.transpose(dcat).astype(BF)
-    forward(1)
+    forward(1, 1)
+    forward(2, 0)
 
     @pl.when(ind < units)
     def _():
@@ -192,8 +210,9 @@
                 psum_s, total_s.at[ind], ag_send, ag_recv, lax.rem(ind + d, ni), gene
             ).start()
 
-    if nz // 2 >= 2:
-        forward(2)
+    forward(2, 1)
+    forward(3, 0)
+    forward(3, 1)
 
     @pl.when(ind < units)
     def _():
@@ -236,8 +255,8 @@
             call_s.at[gene], call_s.at[gene], c_send, c_recv, ind, lax.rem(gene + d, ng)
         ).start()
 
-    if nz // 2 >= 3:
-        forward(3)
+    forward(4, 0)
+    forward(4, 1)
     base = 1.0 - cross_geno[0:1] / (2.0 * n_total)
     b2 = base * base
     b4 = b2 * b2
@@ -257,10 +276,11 @@
     hcat = jnp.concatenate([h1, h2, h3], axis=0).astype(BF)
 
     sel_r, sel_c = iota((ni * 8, TV), 0), iota((ni * 8, TV), 1)
-    sub = lax.rem(sel_r, 8)
-    sel = jnp.where((sub < COV_ROWS) & (sel_c == lax.div(sel_r, 8) * COV_ROWS + sub), 1.0, 0.0)
+    sub = lax.rem(sel_r, 8) - 8 + COV_ROWS
+    sel = jnp.where((sub >= 0) & (sel_c == lax.div(sel_r, 8) * COV_ROWS + sub), 1.0, 0.0)
     sel = sel.astype(BF)
     diag = iota((TV, TV), 0) == iota((TV, TV), 1)
+    extra = jnp.zeros((8, TV), F32)
     for s in range(SLOTS):
         cols = slice(s * TV, s * TV + TV)
         tile_r = gr_s[:, cols]
@@ -270,41 +290,48 @@
         burden = jnp.sum(wc[0:1] * w, axis=1, keepdims=True)
         dosage = jnp.sum(jnp.where(diag, cov_s, 0.0), axis=0, keepdims=True)
         skat = jnp.sum(dosage * w * w, axis=1, keepdims=True)
-        b_hi, b_lo, _ = split3(burden)
-        k_hi, k_lo, _ = split3(skat)
-        ext = dot(sel, cov_s.astype(BF))
-        ext = jnp.where(sub == 4, b_hi, jnp.where(sub == 5, b_lo, ext))
-        ext = jnp.where(sub == 6, k_hi, jnp.where(sub == 7, k_lo, ext))
-        ext_s[s] = ext.reshape(ni, 8, TV)
-
-    for step in range(4, nz // 2 + 1):
-        forward(step)
+        extra = jnp.where(sub8 == s, burden, jnp.where(sub8 == SLOTS + s, skat, extra))
+        ext_s[s] = dot(sel, cov_s.astype(BF)).reshape(ni, 8, TV)
+    kx_all[0] = extra
+
+    @pl.loop(1, ni)
+    def _(d):
+        remote(
+            kx_all.at[0], kx_all.at[ni - d], k_send, k_recv, lax.rem(ind + d, ni), gene
+        ).start()
+
     got = call_s.at[pl.ds(0, ng - 1)]
     remote(got, got, c_send, c_recv, ind, gene).wait_recv()
-    own_copy.wait_recv()
+    for q in range(2):
+        own_copy(q).wait_recv()
     for step in range(1, nz // 2 + 1):
         for way, q in moves(step):
             across(way, step, q).wait_recv()
 
-    p_s[...] = jnp.zeros_like(p_s)
-
-    @pl.loop(0, ng)
-    def _(j):
-        cj = call_s[j]
-        fix = dot(jnp.concatenate([cj, cj, cj], axis=0), hcat, "tn")
-        p_s[0:pt, :] = (
-            dot(tall[j, 0], gr_s[0:half_rows, :])
-            + dot(tall[j, 1], gr_s[half_rows:, :])
-            - fix[0:pt]
-        )
-        for kk in range(per_chunk):
-            i = j * per_chunk + kk
-            for s in range(SLOTS):
-                part = p_s[kk * half : kk * half + ROWS, s * TV : s * TV + TV]
-                sbuf[s, i] = jnp.concatenate([part, ext_s[s, i]], axis=0).astype(BF)
+    def part_of_scores(pair):
+        cols = slice(pair * PAIR * TV, (pair + 1) * PAIR * TV)
+        chunks = unit_rows // padded
+
+        @pl.loop(0, NX)
+        def _(u):
+            at = pl.ds(pl.multiple_of(u * unit_rows, unit_rows), unit_rows)
+            p_s[...] = dot(tall[0, at, :], gr_s[0:half_rows, cols]) + dot(
+                tall[1, at, :], gr_s[half_rows:, cols]
+            )
+            for c in range(chunks):
+                cj = call_s[u * chunks + c]
+                fix = dot(jnp.concatenate([cj, cj, cj], axis=0), hcat[:, cols], "tn")
+                p_s[c * padded : (c + 1) * padded, :] -= fix[0:padded]
+            for k in range(PAIR):
+                s = pair * PAIR + k
+                lanes_k = slice(k * TV, k * TV + TV)
+                for b in range(ny):
+                    last = slice(b * ROWS + ROWS - 8, b * ROWS + ROWS)
+                    p_s[last, lanes_k] += ext_s[s, u * ny + b]
+                sbuf[s, u] = p_s[:, lanes_k].astype(BF)
 
     def unit(s, to):
-        return sbuf.at[s, pl.ds(lax.rem(to + NX, NX) * ny, ny)]
+        return sbuf.at[s, lax.rem(to + NX, NX)]
 
     def x_copy(s, which):
         sign = 1 if s % 2 == 0 else -1
@@ -323,41 +350,57 @@
             yout.at[s, to], yin.at[s, ny - d], y_send.at[s], y_recv.at[s], x * ny + to, gene
         )
 
+    def start(s):
+        x_copy(s, 0).start()
+        x_copy(s, 1).start()
+
+    both = 2 * ROWS
+
     def relay(s):
         sign = 1 if s % 2 == 0 else -1
         x_copy(s, 0).wait_recv()
-        to = lax.rem(x + sign + NX, NX) * ny
-
-        @pl.loop(0, ny)
+        to = lax.rem(x + sign + NX, NX)
+
+        @pl.loop(0, ny // 2)
         def _(b):
-            relay_out[s, b] = (relay_in[s, b].astype(F32) + sbuf[s, to + b].astype(F32)).astype(BF)
+            at = pl.ds(pl.multiple_of(b * both, both), both)
+            relay_out[s, at, :] = (
+                relay_in[s, at, :].astype(F32) + sbuf[s, to, at, :].astype(F32)
+            ).astype(BF)
 
         x_copy(s, 2).start()
 
     def over_x(s, b):
+        at = pl.ds(pl.multiple_of(b * both, both), both)
         return (
-            sbuf[s, x * ny + b].astype(F32)
-            + from_one[s, b].astype(F32)
-            + from_two[s, b].astype(F32)
+            sbuf[s, x, at, :].astype(F32)
+            + from_one[s, at, :].astype(F32)
+            + from_two[s, at, :].astype(F32)
         )
 
     def gather_x(s):
         x_copy(s, 1).wait_recv()
         x_copy(s, 2).wait_recv()
-
-        @pl.loop(0, ny)
+        pad = jnp.zeros((BLOCK - ROWS, TV), F32)
+
+        @pl.loop(0, ny // 2)
         def _(b):
-            yout[s, b] = over_x(s, b).astype(BF)
+            v = over_x(s, b)
+            yout[s, 2 * b] = jnp.concatenate([v[:ROWS], pad], axis=0).astype(BF)
+            yout[s, 2 * b + 1] = jnp.concatenate([v[ROWS:], pad], axis=0).astype(BF)
 
         @pl.loop(1, ny)
         def _(d):
             y_copy(s, d).start()
 
-    for s in range(SLOTS):
-        x_copy(s, 0).start()
-        x_copy(s, 1).start()
+    part_of_scores(0)
+    start(0)
+    start(1)
+    part_of_scores(1)
     relay(0)
+    start(2)
     relay(1)
+    start(3)
     gather_x(0)
     relay(2)
     gather_x(1)
@@ -369,26 +412,29 @@
     vrow = jnp.broadcast_to(vrow[0:1] + vrow[1:2] + vrow[2:3], (8, TV))
     var = vrow
     for kk in range(1, per_chunk):
-        var = jnp.where(lax.rem(ind, per_chunk) == kk, pltpu.roll(vrow, TV - kk * half, 1), var)
+        var = jnp.where(lax.rem(ind, per_chunk) == kk, pltpu.roll(vrow, TV - kk * ROWS, 1), var)
     var = var[0:1, 0:ROWS]
+    got = kx_all.at[pl.ds(1, ni - 1)]
+    remote(got, got, k_send, k_recv, ind, gene).wait_recv()
+    dens = 1.0 + jnp.sum(kx_all[...], axis=0)
     fin_s[...] = jnp.zeros_like(fin_s)
     for s in range(SLOTS):
         got = yin.at[s, pl.ds(1, ny - 1)]
         remote(got, got, y_send.at[s], y_recv.at[s], ind, gene).wait_recv()
-        whole = over_x(s, y)
+        v = over_x(s, lax.div(y, 2))
+        whole = jnp.where(lax.rem(y, 2) == 0, v[:ROWS], v[ROWS:])
         for d in range(1, ny):
-            whole = whole + yin[s, d].astype(F32)
-        score = whole[0:ROWS]
+            whole = whole + yin[s, d].astype(F32)[:ROWS]
         w = jnp.broadcast_to(weight[:, s * TV : s * TV + TV], (8, TV))
-        burden = dot(w, score, "nt", HIGHEST)[0:1]
-        skat = dot(w * w, score * score, "nt", HIGHEST)[0:1]
-        b_den = 1.0 + whole[60:61, 0:ROWS] + whole[61:62, 0:ROWS]
-        k_den = 1.0 + whole[62:63, 0:ROWS] + whole[63:64, 0:ROWS]
+        burden = dot(w, whole, "nt", HIGHEST)[0:1]
+        skat = dot(w * w, whole * whole, "nt", HIGHEST)[0:1]
+        b_den = dens[s : s + 1, 0:ROWS]
+        k_den = dens[SLOTS + s : SLOTS + s + 1, 0:ROWS]
         fin_s[s : s + 1, 0:ROWS] = burden / jnp.sqrt(b_den * var)
         fin_s[4 + s : 5 + s, 0:ROWS] = skat / (k_den * var)
         up = 4 * (s // 2)
         left = TV + TV * (s % 2)
-        fin_s[up : up + 4, left : left + TV] = whole[56:60] * (1.0 / n_total)
+        fin_s[up : up + 4, left : left + TV] = whole[ROWS - COV_ROWS : ROWS] * (1.0 / n_total)
 
     @pl.loop(1, ng)
     def _(d):
@@ -411,7 +457,8 @@
         for way, q in moves(step):
             ring(way, step, q).wait_send()
             across(way, step, q).wait_send()
-    own_copy.wait_send()
+    for q in range(2):
+        own_copy(q).wait_send()
 
     @pl.when(ind < units)
     def _():
@@ -426,6 +473,8 @@
 
     got = call_s.at[pl.ds(0, ng - 1)]
     remote(got, got, c_send, c_recv, ind, gene).wait_send()
+    got = kx_all.at[pl.ds(1, ni - 1)]
+    remote(got, got, k_send, k_recv, ind, gene).wait_send()
     for s in range(SLOTS):
         for which in range(3):
             x_copy(s, which).wait_send()
@@ -489,7 +538,9 @@
     ny, nz = ni // NX, ng // 2
     vmem = pl.BlockSpec(memory_space=pltpu.VMEM)
     dma = pltpu.SemaphoreType.DMA
-    unit = (SLOTS, ny, BLOCK, TV)
+    unit = (SLOTS, ny * ROWS, TV)
+    block = (SLOTS, ny, BLOCK, TV)
+    padded = ni // ng * ROWS
     scratch = [
         pltpu.VMEM((rows, lanes), jnp.int32),
         pltpu.VMEM((rows, lanes), BF),
@@ -497,30 +548,31 @@
         pltpu.VMEM((32, rows), F32),
         pltpu.VMEM((96, rows), BF),
         pltpu.VMEM((rows, 256), BF),
-        pltpu.VMEM((ng, 2, pt, rows // 2), BF),
+        pltpu.VMEM((2, ng * padded, rows // 2), BF),
         pltpu.VMEM((units, tall_unit, TV), F32),
         pltpu.VMEM((ni, tall_unit, TV), F32),
         pltpu.VMEM((tall_unit, TV), F32),
         pltpu.VMEM((units, tall_unit, TV), F32),
         pltpu.VMEM((ng, 32, TV), BF),
         pltpu.VMEM((SLOTS, ni, 8, TV), F32),
-        pltpu.VMEM((112, lanes), F32),
-        pltpu.VMEM((SLOTS, ni, BLOCK, TV), BF),
+        pltpu.VMEM((ni, 8, TV), F32),
+        pltpu.VMEM((ny * ROWS, PAIR * TV), F32),
+        pltpu.VMEM((SLOTS, NX, ny * ROWS, TV), BF),
         pltpu.VMEM(unit, BF),
         pltpu.VMEM(unit, BF),
         pltpu.VMEM(unit, BF),
         pltpu.VMEM(unit, BF),
-        pltpu.VMEM(unit, BF),
-        pltpu.VMEM(unit, BF),
+        pltpu.VMEM(block, BF),
+        pltpu.VMEM(block, BF),
         pltpu.VMEM((8, 3 * TV), F32),
         pltpu.VMEM((ng, 8, 3 * TV), F32),
         dma,
         dma((2, nz // 2, 2)), dma((2, nz // 2, 2)),
         dma((2, nz // 2, 2)), dma((2, nz // 2, 2)),
-        dma, dma, dma, dma, dma, dma, dma, dma,
+        dma((2,)), dma((2,)), dma, dma, dma, dma, dma, dma,
         dma((SLOTS, 3)), dma((SLOTS, 3)),
         dma((SLOTS,)), dma((SLOTS,)),
-        dma, dma,
+        dma, dma, dma, dma,
     ]
     return pl.pallas_call(
         functools.partial(kernel, ni, ng, half, units),

time: 90.2 us -> 83.5 us (0.926)
  Pallas kernels: 85.6 us -> 78.9 us
    pallas_call x1, Pallas kernels: 85.6 us -> 78.9 us  [per_device(): pl.pallas_call(functools.partial(kernel, ni, ng, half, units), out_shape=...]
where the time goes in v3:
time: 83.5 us; the launch traced here: 83.3 us
  Pallas kernels  78.9 us (94%)
  local copies, waits for them, and re-layouts  3.71 us (4%)
    pallas_call x1, Pallas kernels, per_device(): pl.pallas_call(functools.partial(kernel, ni, ng, half, units), out_shape=...  78.9 us
    unnamed x3, local copies, waits for them, and re-layouts  3.71 us

profile of v3, /device:TPU:1, one launch (start us, length us, event | category | flops | bytes accessed | tf_op | source)
XLA Modules:
  0.0 83.3 jit_solution(11802452852064020831)
XLA Ops:
  0.6 78.9 %shard_map.76 = (f32[2,52]{1,0:T(2,128)}, f32[2,52]{1,0:T(2,128)}, f32[2,4,128]{2,1,0:T(4,128)}) custom-call(s32[1024,512]{1,0:T(8,128)} %geno_ref.1, f32[20,1024]{1,0:T(8,128)} %cov_ref.1, bf16[104,1024]{1,0:T(8,128)(2,1)} %bitcast.3, s32[1,32]{1,0:T(1,128)} %bitcast.4, s32[1,32]{1,0:T(1,128)} %bitcast.5), custom_call_target="tpu_custom_call" | custom-call | tf_op jit(solution)/shard_map/pallas_call | solution.py:577
  79.6 1.2 %copy.11 = f32[2,52]{1,0:T(2,128)} copy(f32[2,52]{1,0:T(2,128)} %get-tuple-element.6) | data formatting | bytes 832
  80.8 1.2 %copy.12 = f32[2,52]{1,0:T(2,128)} copy(f32[2,52]{1,0:T(2,128)} %get-tuple-element.7) | data formatting | bytes 832
  82.0 1.3 %copy.13 = f32[2,4,128]{2,1,0:T(4,128)} copy(f32[2,4,128]{2,1,0:T(4,128)} %get-tuple-element.8) | data formatting | bytes 8192

commit v4 on v3

--- a/solution.py
+++ b/solution.py
@@ -13,7 +13,6 @@
 SLOTS = 4
 NX = 4
 ROWS = 56
-BLOCK = 64
 PAIR = 2
 COV_ROWS = 4
 TILES = 18
@@ -85,27 +84,20 @@
             barrier, inc=1, device_id=(ind, lax.rem(gene + d, ng)), device_id_type=MESH
         )
 
-    spread_r, spread_c = iota((padded, pt), 0), iota((padded, pt), 1)
-    spread = spread_r - spread_r // ROWS * (ROWS - half) == spread_c
-    spread = jnp.where(spread & (spread_r % ROWS < half), 1.0, 0.0).astype(BF)
-    tall_own = dot(spread, prot_ref[...]).astype(BF)
-    own_rows = pl.ds(pl.multiple_of(gene * padded, padded), padded)
-    tall[0, own_rows, :] = tall_own[:, :half_rows]
-    tall[1, own_rows, :] = tall_own[:, half_rows:]
-    mask, pick = selections(home_ref[...], len_ref[...], gene, ng)
     pl.semaphore_wait(barrier, ni + ng - 2)
 
     def chunk_of(way, step):
         sign = 1 if way == 0 else -1
         chunk = lax.rem(z - sign * step + 2 * nz, nz) * 2 + core
-        return pl.ds(pl.multiple_of(chunk * padded, padded), padded)
+        return pl.ds(pl.multiple_of(chunk * padded, padded), pt)
 
     def ring(way, step, q):
         sign = 1 if way == 0 else -1
         block = tall.at[q, chunk_of(way, step - 1)]
+        source = block if step > 1 else prot_ref.at[:, pl.ds(q * half_rows, half_rows)]
         target = lax.rem(z + sign + nz, nz) * 2 + core
         return remote(
-            block, block, t_send.at[way, step - 1, q], t_recv.at[way, step - 1, q], ind, target
+            source, block, t_send.at[way, step - 1, q], t_recv.at[way, step - 1, q], ind, target
         )
 
     def across(way, step, q):
@@ -120,14 +112,21 @@
             return [(way, q) for q in range(2) for way in range(2)]
         return [(0, 0), (1, 1)]
 
+    own_rows = pl.ds(pl.multiple_of(gene * padded, padded), pt)
+
     def own_copy(q):
+        source = prot_ref.at[:, pl.ds(q * half_rows, half_rows)]
         block = tall.at[q, own_rows]
-        return remote(block, block, own_send.at[q], own_recv.at[q], ind, z * 2 + 1 - core)
+        return remote(source, block, own_send.at[q], own_recv.at[q], ind, z * 2 + 1 - core)
 
     for way, q in moves(1):
         ring(way, 1, q).start()
     for q in range(2):
         own_copy(q).start()
+    tall_own = prot_ref[...]
+    tall[0, own_rows, :] = tall_own[:, :half_rows]
+    tall[1, own_rows, :] = tall_own[:, half_rows:]
+    mask, pick = selections(home_ref[...], len_ref[...], gene, ng)
 
     def forward(step, half_of):
         if step > nz // 2:
@@ -162,7 +161,7 @@
     sq_lo = (square - sq_hi.astype(F32)).astype(BF)
     ones = jnp.ones((16, rows), BF)
     t2 = dot(ones, sq_hi, "nt") + dot(ones, sq_lo, "nt")
-    dt = dt[0:24] + jnp.where(iota((24, padded), 0) == WIDTH, t2[0:1], 0.0)
+    dt = dt[0:24] + jnp.where(iota((24, pt), 0) == WIDTH, t2[0:1], 0.0)
     gram = dot(design, design, "nt", HIGHEST)
     stat_s[...] = jnp.zeros_like(stat_s)
     for r in range(3):
@@ -173,7 +172,7 @@
             stat_s[k // per_unit, at, :] = dg[sub, TV * c : TV * c + TV]
         k = 12 + r
         at = slice(8 * (k % per_unit), 8 * (k % per_unit) + 8)
-        stat_s[k // per_unit, at, 0:padded] = dt[sub]
+        stat_s[k // per_unit, at, 0:pt] = dt[sub]
         k = 15 + r
         at = slice(8 * (k % per_unit), 8 * (k % per_unit) + 8)
         stat_s[k // per_unit, at, 0:32] = gram[sub]
@@ -325,10 +324,13 @@
             for k in range(PAIR):
                 s = pair * PAIR + k
                 lanes_k = slice(k * TV, k * TV + TV)
+                blocks = []
                 for b in range(ny):
-                    last = slice(b * ROWS + ROWS - 8, b * ROWS + ROWS)
-                    p_s[last, lanes_k] += ext_s[s, u * ny + b]
-                sbuf[s, u] = p_s[:, lanes_k].astype(BF)
+                    low = b // per_chunk * padded + b % per_chunk * half
+                    blocks.append(p_s[low : low + ROWS - 8, lanes_k])
+                    end = p_s[low + ROWS - 8 : low + ROWS, lanes_k]
+                    blocks.append(jnp.where(sub8 < 8 - COV_ROWS, end, ext_s[s, u * ny + b]))
+                sbuf[s, u] = jnp.concatenate(blocks, axis=0).astype(BF)
 
     def unit(s, to):
         return sbuf.at[s, lax.rem(to + NX, NX)]
@@ -381,17 +383,38 @@
     def gather_x(s):
         x_copy(s, 1).wait_recv()
         x_copy(s, 2).wait_recv()
-        pad = jnp.zeros((BLOCK - ROWS, TV), F32)
 
         @pl.loop(0, ny // 2)
         def _(b):
             v = over_x(s, b)
-            yout[s, 2 * b] = jnp.concatenate([v[:ROWS], pad], axis=0).astype(BF)
-            yout[s, 2 * b + 1] = jnp.concatenate([v[ROWS:], pad], axis=0).astype(BF)
+            yout[s, 2 * b] = v[:ROWS].astype(BF)
+            yout[s, 2 * b + 1] = v[ROWS:].astype(BF)
 
         @pl.loop(1, ny)
         def _(d):
             y_copy(s, d).start()
+
+    def finish(s, var, dens):
+        got = yin.at[s, pl.ds(1, ny - 1)]
+        remote(got, got, y_send.at[s], y_recv.at[s], ind, gene).wait_recv()
+        v = over_x(s, lax.div(y, 2))
+        whole = jnp.where(lax.rem(y, 2) == 0, v[:ROWS], v[ROWS:])
+        for d in range(1, ny):
+            whole = whole + yin[s, d].astype(F32)
+        w = jnp.broadcast_to(weight[:, s * TV : s * TV + TV], (8, TV))
+        burden = dot(w, whole, "nt", HIGHEST)[0:1]
+        skat = dot(w * w, whole * whole, "nt", HIGHEST)[0:1]
+        fin_s[s, 0:COV_ROWS, :] = whole[ROWS - COV_ROWS : ROWS] * (1.0 / n_total)
+        fin_s[s, 4:5, 0:ROWS] = burden / jnp.sqrt(dens[s : s + 1, 0:ROWS] * var)
+        fin_s[s, 5:6, 0:ROWS] = skat / (dens[SLOTS + s : SLOTS + s + 1, 0:ROWS] * var)
+        fall[s, 0] = fin_s[s]
+
+        @pl.loop(1, ng)
+        def _(d):
+            remote(
+                fin_s.at[s], fall.at[s, ng - d], f_send.at[s], f_recv.at[s],
+                ind, lax.rem(gene + d, ng),
+            ).start()
 
     part_of_scores(0)
     start(0)
@@ -401,57 +424,33 @@
     start(2)
     relay(1)
     start(3)
+    fin_s[...] = jnp.zeros_like(fin_s)
+    vrow = call_s[lax.div(ind, per_chunk)].astype(F32)[24:32]
+    vrow = jnp.broadcast_to(vrow[0:1] + vrow[1:2] + vrow[2:3], (8, TV))
+    var = vrow
+    for kk in range(1, per_chunk):
+        var = jnp.where(lax.rem(ind, per_chunk) == kk, pltpu.roll(vrow, TV - kk * half, 1), var)
+    var = var[0:1, 0:ROWS]
+    got = kx_all.at[pl.ds(1, ni - 1)]
+    remote(got, got, k_send, k_recv, ind, gene).wait_recv()
+    dens = 1.0 + jnp.sum(kx_all[...], axis=0)
     gather_x(0)
     relay(2)
     gather_x(1)
     relay(3)
     gather_x(2)
+    finish(0, var, dens)
     gather_x(3)
-
-    vrow = call_s[lax.div(ind, per_chunk)].astype(F32)[24:32]
-    vrow = jnp.broadcast_to(vrow[0:1] + vrow[1:2] + vrow[2:3], (8, TV))
-    var = vrow
-    for kk in range(1, per_chunk):
-        var = jnp.where(lax.rem(ind, per_chunk) == kk, pltpu.roll(vrow, TV - kk * ROWS, 1), var)
-    var = var[0:1, 0:ROWS]
-    got = kx_all.at[pl.ds(1, ni - 1)]
-    remote(got, got, k_send, k_recv, ind, gene).wait_recv()
-    dens = 1.0 + jnp.sum(kx_all[...], axis=0)
-    fin_s[...] = jnp.zeros_like(fin_s)
+    for s in range(1, SLOTS):
+        finish(s, var, dens)
     for s in range(SLOTS):
-        got = yin.at[s, pl.ds(1, ny - 1)]
-        remote(got, got, y_send.at[s], y_recv.at[s], ind, gene).wait_recv()
-        v = over_x(s, lax.div(y, 2))
-        whole = jnp.where(lax.rem(y, 2) == 0, v[:ROWS], v[ROWS:])
-        for d in range(1, ny):
-            whole = whole + yin[s, d].astype(F32)[:ROWS]
-        w = jnp.broadcast_to(weight[:, s * TV : s * TV + TV], (8, TV))
-        burden = dot(w, whole, "nt", HIGHEST)[0:1]
-        skat = dot(w * w, whole * whole, "nt", HIGHEST)[0:1]
-        b_den = dens[s : s + 1, 0:ROWS]
-        k_den = dens[SLOTS + s : SLOTS + s + 1, 0:ROWS]
-        fin_s[s : s + 1, 0:ROWS] = burden / jnp.sqrt(b_den * var)
-        fin_s[4 + s : 5 + s, 0:ROWS] = skat / (k_den * var)
-        up = 4 * (s // 2)
-        left = TV + TV * (s % 2)
-        fin_s[up : up + 4, left : left + TV] = whole[ROWS - COV_ROWS : ROWS] * (1.0 / n_total)
-
-    @pl.loop(1, ng)
-    def _(d):
-        remote(fin_s, fall.at[ng - d], f_send, f_recv, ind, lax.rem(gene + d, ng)).start()
-
-    fall[0] = fin_s[...]
-    got = fall.at[pl.ds(1, ng - 1)]
-    remote(got, got, f_send, f_recv, ind, gene).wait_recv()
-    flat = fall[...].reshape(ng * 8, 3 * TV)
-    stats = dot(pick[0:8], flat[:, 0:TV], "nn", HIGHEST)
-    bz_ref[...] = stats[0:2, 0:half]
-    sq_ref[...] = stats[2:4, 0:half]
-    cov_out = dot(pick[8:16], flat[:, TV : 2 * TV], "nn", HIGHEST) + dot(
-        pick[16:24], flat[:, 2 * TV :], "nn", HIGHEST
-    )
-    cv_ref[0] = cov_out[0:4]
-    cv_ref[1] = cov_out[4:8]
+        got = fall.at[s, pl.ds(1, ng - 1)]
+        remote(got, got, f_send.at[s], f_recv.at[s], ind, gene).wait_recv()
+    mine = dot(pick, fall[...].reshape(SLOTS * ng * 8, TV), "nn", HIGHEST)
+    bz_ref[...] = mine[0:2, 0:half]
+    sq_ref[...] = mine[2:4, 0:half]
+    cv_ref[0] = mine[8:12]
+    cv_ref[1] = mine[12:16]
 
     for step in range(1, nz // 2 + 1):
         for way, q in moves(step):
@@ -480,8 +479,9 @@
             x_copy(s, which).wait_send()
         got = yout.at[s, pl.ds(0, ny - 1)]
         remote(got, got, y_send.at[s], y_recv.at[s], ind, gene).wait_send()
-    got = fall.at[pl.ds(1, ng - 1)]
-    remote(got, got, f_send, f_recv, ind, gene).wait_send()
+    for s in range(SLOTS):
+        got = fall.at[s, pl.ds(1, ng - 1)]
+        remote(got, got, f_send.at[s], f_recv.at[s], ind, gene).wait_send()
 
 
 def selections(home, length, me, ng):
@@ -511,20 +511,13 @@
     far = jnp.where(far < 0, far + ng, far)
     here = [chosen(gene_id == me * owned + o, far) for o in range(owned)]
     slot = [chosen(gene_id == me * owned + o, rank) for o in range(owned)]
-    r, c = iota((24, ng * 8), 0), iota((24, ng * 8), 1)
-    first = jnp.where(r < 8, r % 2, (r - 8) % 8 // 4) == 0
+    r, c = iota((16, SLOTS * ng * 8), 0), iota((16, SLOTS * ng * 8), 1)
+    first = jnp.where(r < 8, r % 2, (r - 8) // 4) == 0
     at = jnp.where(first, here[0], here[1])
     s = jnp.where(first, slot[0], slot[1])
-    upper = jnp.where(s < 2, 0, 1)
-    stat_col = at * 8 + jnp.where(r < 2, s, 4 + s)
-    cov_col = at * 8 + upper * 4 + (r - 8) % 4
-    cov_on = (s - upper * 2) == (r - 8) // 8
-    hit = jnp.where(
-        r < 8,
-        jnp.where((c == stat_col) & (r < 4), 1.0, 0.0),
-        jnp.where((c == cov_col) & cov_on, 1.0, 0.0),
-    )
-    return mask, hit
+    line = jnp.where(r < 8, jnp.where(r < 2, 4, 5), r % 4)
+    hit = (c == (s * ng + at) * 8 + line) & ((r < 4) | (r >= 8))
+    return mask, jnp.where(hit, 1.0, 0.0)
 
 
 def per_device(genotypes, covariates, proteins, gene_device, tile_len):
@@ -539,7 +532,7 @@
     vmem = pl.BlockSpec(memory_space=pltpu.VMEM)
     dma = pltpu.SemaphoreType.DMA
     unit = (SLOTS, ny * ROWS, TV)
-    block = (SLOTS, ny, BLOCK, TV)
+    block = (SLOTS, ny, ROWS, TV)
     padded = ni // ng * ROWS
     scratch = [
         pltpu.VMEM((rows, lanes), jnp.int32),
@@ -564,15 +557,15 @@
         pltpu.VMEM(unit, BF),
         pltpu.VMEM(block, BF),
         pltpu.VMEM(block, BF),
-        pltpu.VMEM((8, 3 * TV), F32),
-        pltpu.VMEM((ng, 8, 3 * TV), F32),
+        pltpu.VMEM((SLOTS, 8, TV), F32),
+        pltpu.VMEM((SLOTS, ng, 8, TV), F32),
         dma,
         dma((2, nz // 2, 2)), dma((2, nz // 2, 2)),
         dma((2, nz // 2, 2)), dma((2, nz // 2, 2)),
         dma((2,)), dma((2,)), dma, dma, dma, dma, dma, dma,
         dma((SLOTS, 3)), dma((SLOTS, 3)),
         dma((SLOTS,)), dma((SLOTS,)),
-        dma, dma, dma, dma,
+        dma, dma, dma((SLOTS,)), dma((SLOTS,)),
     ]
     return pl.pallas_call(
         functools.partial(kernel, ni, ng, half, units),

time: 83.5 us -> 81.3 us (0.974)
  Pallas kernels: 78.9 us -> 76.7 us
    pallas_call x1, Pallas kernels: 78.9 us -> 76.7 us  [per_device(): pl.pallas_call(functools.partial(kernel, ni, ng, half, units), out_shape=...]
where the time goes in v4:
time: 81.3 us; the launch traced here: 81.1 us
  Pallas kernels  76.7 us (94%)
  local copies, waits for them, and re-layouts  3.71 us (5%)
    pallas_call x1, Pallas kernels, per_device(): pl.pallas_call(functools.partial(kernel, ni, ng, half, units), out_shape=...  76.7 us
    unnamed x3, local copies, waits for them, and re-layouts  3.71 us

profile of v4, /device:TPU:1, one launch (start us, length us, event | category | flops | bytes accessed | tf_op | source)
XLA Modules:
  0.0 81.1 jit_solution(15147324060730325559)
XLA Ops:
  0.6 76.7 %shard_map.76 = (f32[2,52]{1,0:T(2,128)}, f32[2,52]{1,0:T(2,128)}, f32[2,4,128]{2,1,0:T(4,128)}) custom-call(s32[1024,512]{1,0:T(8,128)} %geno_ref.1, f32[20,1024]{1,0:T(8,128)} %cov_ref.1, bf16[104,1024]{1,0:T(8,128)(2,1)} %bitcast.3, s32[1,32]{1,0:T(1,128)} %bitcast.4, s32[1,32]{1,0:T(1,128)} %bitcast.5), custom_call_target="tpu_custom_call" | custom-call | tf_op jit(solution)/shard_map/pallas_call | solution.py:570
  77.4 1.2 %copy.11 = f32[2,52]{1,0:T(2,128)} copy(f32[2,52]{1,0:T(2,128)} %get-tuple-element.6) | data formatting | bytes 832
  78.6 1.2 %copy.12 = f32[2,52]{1,0:T(2,128)} copy(f32[2,52]{1,0:T(2,128)} %get-tuple-element.7) | data formatting | bytes 832
  79.8 1.3 %copy.13 = f32[2,4,128]{2,1,0:T(4,128)} copy(f32[2,4,128]{2,1,0:T(4,128)} %get-tuple-element.8) | data formatting | bytes 8192

commit v5 on v4

--- a/solution.py
+++ b/solution.py
@@ -14,6 +14,7 @@
 NX = 4
 ROWS = 56
 PAIR = 2
+X_FIRST = 3
 COV_ROWS = 4
 TILES = 18
 
@@ -43,9 +44,9 @@
     ni, ng, half, units,
     geno_ref, cov_ref, prot_ref, home_ref, len_ref,
     bz_ref, sq_ref, cv_ref,
-    g_s, gb_s, gr_s, d_s, dst_s, dct_s, tall, stat_s, part_s, psum_s, total_s, call_s,
+    s3, r_in, r_out, l_in, l_out, x3_out, x3_in, g_s, gb_s, gr_s, d_s, dst_s, dct_s, tall, stat_s, part_s, psum_s, total_s, call_s,
     ext_s, kx_all, p_s, sbuf, relay_in, relay_out, from_one, from_two, yout, yin, fin_s, fall,
-    load_sem, t_send, t_recv, pair_send, pair_recv, own_send, own_recv,
+    r_send, r_recv, l_send, l_recv, x3_send, x3_recv, load_sem, t_send, t_recv, pair_send, pair_recv, own_send, own_recv,
     rs_send, rs_recv, ag_send, ag_recv, c_send, c_recv, x_send, x_recv, y_send, y_recv,
     k_send, k_recv, f_send, f_recv,
 ):
@@ -330,7 +331,12 @@
                     blocks.append(p_s[low : low + ROWS - 8, lanes_k])
                     end = p_s[low + ROWS - 8 : low + ROWS, lanes_k]
                     blocks.append(jnp.where(sub8 < 8 - COV_ROWS, end, ext_s[s, u * ny + b]))
-                sbuf[s, u] = jnp.concatenate(blocks, axis=0).astype(BF)
+                if s < X_FIRST:
+                    sbuf[s, u] = jnp.concatenate(blocks, axis=0).astype(BF)
+                else:
+                    for b in range(ny):
+                        pair_of = jnp.concatenate(blocks[2 * b : 2 * b + 2], axis=0)
+                        s3[b, u] = pair_of.astype(BF)
 
     def unit(s, to):
         return sbuf.at[s, lax.rem(to + NX, NX)]
@@ -394,13 +400,72 @@
         def _(d):
             y_copy(s, d).start()
 
+    far = ny // 2
+
+    def at_y(k):
+        return lax.rem(y + k + ny, ny)
+
+    def y_right(t):
+        source = s3.at[at_y(far)] if t == 1 else r_out.at[t - 2]
+        to = x * ny + at_y(1)
+        return remote(source, r_in.at[t - 1], r_send.at[t - 1], r_recv.at[t - 1], to, gene)
+
+    def y_left(t):
+        source = s3.at[at_y(1 - far)] if t == 1 else l_out.at[t - 2]
+        to = x * ny + at_y(-1)
+        return remote(source, l_in.at[t - 1], l_send.at[t - 1], l_recv.at[t - 1], to, gene)
+
+    def y_step(t):
+        if t <= far:
+            if t > 1:
+                y_right(t - 1).wait_recv()
+                r_out[t - 2] = (
+                    r_in[t - 2].astype(F32) + s3[at_y(far + 1 - t)].astype(F32)
+                ).astype(BF)
+            y_right(t).start()
+        if t < far:
+            if t > 1:
+                y_left(t - 1).wait_recv()
+                l_out[t - 2] = (
+                    l_in[t - 2].astype(F32) + s3[at_y(t - far)].astype(F32)
+                ).astype(BF)
+            y_left(t).start()
+
+    def over_y(k):
+        total = s3[y, k].astype(F32) + r_in[far - 1, k].astype(F32)
+        return total + l_in[far - 2, k].astype(F32) if far > 1 else total
+
+    def x3_copy(d):
+        to = lax.rem(x + d, NX)
+        return remote(x3_out.at[to], x3_in.at[NX - d], x3_send, x3_recv, to * ny + y, gene)
+
+    def gather_y():
+        y_right(far).wait_recv()
+        if far > 1:
+            y_left(far - 1).wait_recv()
+        for k in range(NX):
+            x3_out[k] = over_y(k).astype(BF)
+        for d in range(1, NX):
+            x3_copy(d).start()
+
+    def whole_of(s):
+        if s < X_FIRST:
+            got = yin.at[s, pl.ds(1, ny - 1)]
+            remote(got, got, y_send.at[s], y_recv.at[s], ind, gene).wait_recv()
+            v = over_x(s, lax.div(y, 2))
+            whole = jnp.where(lax.rem(y, 2) == 0, v[:ROWS], v[ROWS:])
+            for d in range(1, ny):
+                whole = whole + yin[s, d].astype(F32)
+            return whole
+        got = x3_in.at[pl.ds(1, NX - 1)]
+        remote(got, got, x3_send, x3_recv, ind, gene).wait_recv()
+        whole = over_y(x)
+        for d in range(1, NX):
+            whole = whole + x3_in[d].astype(F32)
+        return whole
+
     def finish(s, var, dens):
-        got = yin.at[s, pl.ds(1, ny - 1)]
-        remote(got, got, y_send.at[s], y_recv.at[s], ind, gene).wait_recv()
-        v = over_x(s, lax.div(y, 2))
-        whole = jnp.where(lax.rem(y, 2) == 0, v[:ROWS], v[ROWS:])
-        for d in range(1, ny):
-            whole = whole + yin[s, d].astype(F32)
+        whole = whole_of(s)
         w = jnp.broadcast_to(weight[:, s * TV : s * TV + TV], (8, TV))
         burden = dot(w, whole, "nt", HIGHEST)[0:1]
         skat = dot(w * w, whole * whole, "nt", HIGHEST)[0:1]
@@ -416,14 +481,14 @@
                 ind, lax.rem(gene + d, ng),
             ).start()
 
+    part_of_scores(1)
+    y_step(1)
+    start(2)
     part_of_scores(0)
     start(0)
+    relay(2)
+    y_step(2)
     start(1)
-    part_of_scores(1)
-    relay(0)
-    start(2)
-    relay(1)
-    start(3)
     fin_s[...] = jnp.zeros_like(fin_s)
     vrow = call_s[lax.div(ind, per_chunk)].astype(F32)[24:32]
     vrow = jnp.broadcast_to(vrow[0:1] + vrow[1:2] + vrow[2:3], (8, TV))
@@ -434,15 +499,18 @@
     got = kx_all.at[pl.ds(1, ni - 1)]
     remote(got, got, k_send, k_recv, ind, gene).wait_recv()
     dens = 1.0 + jnp.sum(kx_all[...], axis=0)
+    relay(0)
+    y_step(3)
+    gather_x(2)
+    relay(1)
+    y_step(4)
     gather_x(0)
-    relay(2)
+    finish(2, var, dens)
+    gather_y()
     gather_x(1)
-    relay(3)
-    gather_x(2)
     finish(0, var, dens)
-    gather_x(3)
-    for s in range(1, SLOTS):
-        finish(s, var, dens)
+    finish(3, var, dens)
+    finish(1, var, dens)
     for s in range(SLOTS):
         got = fall.at[s, pl.ds(1, ng - 1)]
         remote(got, got, f_send.at[s], f_recv.at[s], ind, gene).wait_recv()
@@ -474,7 +542,13 @@
     remote(got, got, c_send, c_recv, ind, gene).wait_send()
     got = kx_all.at[pl.ds(1, ni - 1)]
     remote(got, got, k_send, k_recv, ind, gene).wait_send()
-    for s in range(SLOTS):
+    for t in range(1, far + 1):
+        y_right(t).wait_send()
+        if t < far:
+            y_left(t).wait_send()
+    got = x3_in.at[pl.ds(1, NX - 1)]
+    remote(got, got, x3_send, x3_recv, ind, gene).wait_send()
+    for s in range(X_FIRST):
         for which in range(3):
             x_copy(s, which).wait_send()
         got = yout.at[s, pl.ds(0, ny - 1)]
@@ -535,6 +609,13 @@
     block = (SLOTS, ny, ROWS, TV)
     padded = ni // ng * ROWS
     scratch = [
+        pltpu.VMEM((ny, NX, ROWS, TV), BF),
+        pltpu.VMEM((ny // 2, NX, ROWS, TV), BF),
+        pltpu.VMEM((ny // 2, NX, ROWS, TV), BF),
+        pltpu.VMEM((ny // 2, NX, ROWS, TV), BF),
+        pltpu.VMEM((ny // 2, NX, ROWS, TV), BF),
+        pltpu.VMEM((NX, ROWS, TV), BF),
+        pltpu.VMEM((NX, ROWS, TV), BF),
         pltpu.VMEM((rows, lanes), jnp.int32),
         pltpu.VMEM((rows, lanes), BF),
         pltpu.VMEM((rows, lanes), BF),
@@ -559,6 +640,7 @@
         pltpu.VMEM(block, BF),
         pltpu.VMEM((SLOTS, 8, TV), F32),
         pltpu.VMEM((SLOTS, ng, 8, TV), F32),
+        dma((ny // 2,)), dma((ny // 2,)), dma((ny // 2,)), dma((ny // 2,)), dma, dma,
         dma,
         dma((2, nz // 2, 2)), dma((2, nz // 2, 2)),
         dma((2, nz // 2, 2)), dma((2, nz // 2, 2)),

time: 81.3 us -> 79.1 us (0.973)
  Pallas kernels: 76.7 us -> 74.6 us
    pallas_call x1, Pallas kernels: 76.7 us -> 74.6 us  [per_device(): pl.pallas_call(functools.partial(kernel, ni, ng, half, units), out_shape=...]
where the time goes in v5:
time: 79.1 us; the launch traced here: 78.9 us
  Pallas kernels  74.6 us (94%)
  local copies, waits for them, and re-layouts  3.71 us (5%)
    pallas_call x1, Pallas kernels, per_device(): pl.pallas_call(functools.partial(kernel, ni, ng, half, units), out_shape=...  74.6 us
    unnamed x3, local copies, waits for them, and re-layouts  3.71 us

profile of v5, /device:TPU:1, one launch (start us, length us, event | category | flops | bytes accessed | tf_op | source)
XLA Modules:
  0.0 78.9 jit_solution(10492098599897443775)
XLA Ops:
  0.6 74.6 %shard_map.76 = (f32[2,52]{1,0:T(2,128)}, f32[2,52]{1,0:T(2,128)}, f32[2,4,128]{2,1,0:T(4,128)}) custom-call(s32[1024,512]{1,0:T(8,128)} %geno_ref.1, f32[20,1024]{1,0:T(8,128)} %cov_ref.1, bf16[104,1024]{1,0:T(8,128)(2,1)} %bitcast.3, s32[1,32]{1,0:T(1,128)} %bitcast.4, s32[1,32]{1,0:T(1,128)} %bitcast.5), custom_call_target="tpu_custom_call" | custom-call | tf_op jit(solution)/shard_map/pallas_call | solution.py:652
  75.2 1.2 %copy.11 = f32[2,52]{1,0:T(2,128)} copy(f32[2,52]{1,0:T(2,128)} %get-tuple-element.6) | data formatting | bytes 832
  76.4 1.2 %copy.12 = f32[2,52]{1,0:T(2,128)} copy(f32[2,52]{1,0:T(2,128)} %get-tuple-element.7) | data formatting | bytes 832
  77.7 1.3 %copy.13 = f32[2,4,128]{2,1,0:T(4,128)} copy(f32[2,4,128]{2,1,0:T(4,128)} %get-tuple-element.8) | data formatting | bytes 8192
